TPU v7x, 32 devices: a whole 2x2x4 slice. The times are simulated.
32 devices in a mesh: dp: 4 (over x, core), gate: 8 (over z, y).
Axes of the slice: x: 2, y: 2, z: 4, core: 2. Of those that a mesh axis runs over, the one named last changes fastest.
Arguments:
- frames: bfloat16 [20, 16, 16384], P(None, None, 'dp'), may hold values from -6 to 6
- regions: int32 [16384], P('dp'), may hold values from 0 to 7, as said below
- valid: int32 [15, 16384], P(None, 'dp'), may hold values from 0 to 1, as said below
- step_count: int32 [4], replicated, may hold values from 1 to 20
- conv_w: float32 [2, 4, 128, 1296], P(None, None, 'gate'), may hold values from -0.15625 to 0.15625
- cell_params: float32 [2, 7, 128], P(None, None, 'gate'), may hold values from -3 to 3
- head_w: float32 [16, 128], replicated, may hold values from -0.5 to 0.5
- head_b: float32 [16], replicated, may hold values from -2 to 2
- conv_mom: float32 [2, 4, 128, 1296], P(None, None, 'gate'), may hold values from -0.0009765625 to 0.0009765625
- cell_mom: float32 [2, 7, 128], P(None, None, 'gate'), may hold values from -0.005859375 to 0.005859375
- head_mom: float32 [16, 128], replicated, may hold values from -0.005859375 to 0.005859375
- bias_mom: float32 [16], replicated, may hold values from -0.01171875 to 0.01171875
- conv_avg: float32 [2, 4, 128, 1296], P(None, None, 'gate'), may hold values from -0.15625 to 0.15625
- cell_avg: float32 [2, 7, 128], P(None, None, 'gate'), may hold values from -3 to 3
- head_avg: float32 [16, 128], replicated, may hold values from -0.5 to 0.5
- bias_avg: float32 [16], replicated, may hold values from -2 to 2
Outputs:
- loss: float32 [], replicated
- conv_mom_new: float32 [2, 4, 128, 1296], P(None, None, 'gate')
- conv_avg_new: float32 [2, 4, 128, 1296], P(None, None, 'gate')
- conv_new: float32 [2, 4, 128, 1296], P(None, None, 'gate')
- conv_low: bfloat16 [2, 4, 128, 1296], P(None, None, 'gate')
- cell_mom_new: float32 [2, 7, 128], P(None, None, 'gate')
- cell_avg_new: float32 [2, 7, 128], P(None, None, 'gate')
- cell_new: float32 [2, 7, 128], P(None, None, 'gate')
- cell_low: bfloat16 [2, 7, 128], P(None, None, 'gate')
- head_mom_new: float32 [16, 128], replicated
- head_avg_new: float32 [16, 128], replicated
- head_new: float32 [16, 128], replicated
- head_low: bfloat16 [16, 128], replicated
- bias_mom_new: float32 [16], replicated
- bias_avg_new: float32 [16], replicated
- bias_new: float32 [16], replicated
- bias_low: bfloat16 [16], replicated
Inputs may be any that keep to these rules, and one draw needn't show every extreme that they name: `regions`: each device's canvas of 32 x 128 pixels is cut into four column bands, each cut into an upper and a lower rectangle; pixel ids are 2 x band + (1 if lower); every id 0 to 7 occurs on every canvas, and the first and last row and column of a canvas always differ in id. `valid`: on canvas b of the 4 canvases each value is 1 with probability (20 + (75 * b) // max(3, 1)) / 100, independently.
All inputs are finite; a program needn't handle non-finite values.
Results may differ from a plain program's by a relative error of at most 0.0059.
Values may be sent and summed in bfloat16 or wider, within the bound.
No kernel may reach another device: no remote copies, remote signals or barrier semaphores. Data moves between devices by JAX's collectives and lax.ppermute only.
A program may use at most 256 MiB of HBM per device.

v0:
```python
import jax
import jax.numpy as jnp
from jax import lax
from jax.sharding import PartitionSpec as P

EIN = 5
EOUT = 15
COLS = 128


MU = 0.9
RATE_SCALE = 0.05


def tap_shift(field, off):
    return jnp.roll(field, -off, axis=-1)


def cell_forward(pre, cell_prev, params):
    in_gate = jax.nn.sigmoid(pre[0] + params[4][:, None] * cell_prev)
    forget = jax.nn.sigmoid(pre[1] + params[5][:, None] * cell_prev)
    update = jnp.tanh(pre[3])
    cell_new = forget * cell_prev + in_gate * update
    out_gate = jax.nn.sigmoid(pre[2] + params[6][:, None] * cell_new)
    return (in_gate, forget, update, cell_new, out_gate, jnp.tanh(cell_new))


def nesterov(param, grad, mom, avg, steps_done, rate):
    mom_new = MU * mom + grad
    param_new = param - rate * (grad + MU * mom_new)
    avg_new = avg + (param_new - avg) / (steps_done + 1.0)
    return [mom_new, avg_new, param_new, param_new.astype(jnp.bfloat16)]


def on_device(
    frames,
    regions,
    valid,
    step_count,
    conv_w,
    cell_params,
    head_w,
    head_b,
    conv_mom,
    cell_mom,
    head_mom,
    bias_mom,
    conv_avg,
    cell_avg,
    head_avg,
    bias_avg,
):
    share = conv_w.shape[2]
    chans = frames.shape[1]
    pixels = frames.shape[2]
    wide = head_w.shape[1]
    groups = lax.axis_size("gate")
    offsets = [dr * COLS + dc for dr in (-1, 0, 1) for dc in (-1, 0, 1)]
    masks = jnp.stack([tap_shift(regions, off) == regions for off in offsets]).astype(jnp.bfloat16)
    conv_lowered = conv_w.astype(jnp.bfloat16)
    weights = conv_lowered.reshape(2, 4 * share, 9, chans + wide)
    everyone_w = lax.all_gather(conv_lowered, "gate", axis=2, tiled=True)
    full_w = everyone_w.reshape(2, 4 * wide, 9, chans + wide)
    own_cols = lax.dynamic_slice_in_dim(full_w, chans + lax.axis_index("gate") * share, share, 3)
    head_lowered = head_w.astype(jnp.bfloat16)
    head_own = lax.dynamic_slice_in_dim(head_lowered, lax.axis_index("gate") * share, share, 1)
    live = valid.astype(jnp.float32)
    count = lax.psum(chans * jnp.sum(live), "dp")
    contract_pix = (((1,), (1,)), ((), ()))
    contract_rows = (((0,), (0,)), ((), ()))

    def conv_apply(weights_l, inp):
        total = jnp.zeros((4 * share, pixels), jnp.float32)
        for tap, off in enumerate(offsets):
            total = total + jnp.dot(
                weights_l[:, tap, :],
                tap_shift(inp, off) * masks[tap],
                preferred_element_type=jnp.float32,
            )
        return total

    def layer_forward(layer, hidden, cell, inputs):
        weights_l = weights[layer]
        params = cell_params[layer]

        def step(carry, xs):
            hidden, cell_prev = carry
            inp = jnp.concatenate([xs[0], hidden], 0)
            pre = conv_apply(weights_l, inp).reshape(4, share, pixels) + params[:4, :, None]
            gates = cell_forward(pre, cell_prev, params)
            out_slice = (gates[4] * gates[5]).astype(jnp.bfloat16)
            gathered = lax.all_gather(out_slice, "gate", axis=0, tiled=True)
            if layer == 0:
                return ((gathered, gates[3]), (pre, cell_prev, gathered))
            guess = (
                jnp.dot(head_lowered, gathered, preferred_element_type=jnp.float32)
                + head_b[:, None]
            )
            weighted = xs[2][None, :] * (guess - xs[1].astype(jnp.float32))
            error_sum = jnp.sum(weighted * (guess - xs[1].astype(jnp.float32)))
            slope = (2.0 / count * weighted).astype(jnp.bfloat16)
            return ((gathered, gates[3]), (pre, cell_prev, gathered, slope, error_sum))

        return lax.scan(step, (hidden, cell), inputs)

    def layer_backward(layer, carry, stored):
        weights_l = weights[layer]
        params = cell_params[layer]

        def step(carry, xs):
            grad_hidden, grad_cell, grad_head, grad_bias, weight_acc, param_acc = carry
            pre, cell_prev, hidden_in, frame = (xs[0], xs[1], xs[2], xs[3])
            if layer == 1:
                slope, gathered = (xs[4], xs[5])
                grad_hidden = grad_hidden + lax.dot_general(
                    head_own, slope, contract_rows, preferred_element_type=jnp.float32
                )
                grad_head = grad_head + lax.dot_general(
                    slope, gathered, contract_pix, preferred_element_type=jnp.float32
                )
                grad_bias = grad_bias + jnp.sum(slope.astype(jnp.float32), 1)
            in_gate, forget, update, cell_new, out_gate, squash = cell_forward(
                pre, cell_prev, params
            )
            d_out = grad_hidden * squash * out_gate * (1.0 - out_gate)
            d_cell = (
                grad_cell
                + grad_hidden * out_gate * (1.0 - squash * squash)
                + d_out * params[6][:, None]
            )
            d_in = d_cell * update * in_gate * (1.0 - in_gate)
            d_forget = d_cell * cell_prev * forget * (1.0 - forget)
            d_update = d_cell * in_gate * (1.0 - update * update)
            cell_back = d_cell * forget + d_in * params[4][:, None] + d_forget * params[5][:, None]
            d_pre = jnp.stack([d_in, d_forget, d_out, d_update])
            peeps = jnp.stack(
                [
                    jnp.sum(d_in * cell_prev, 1),
                    jnp.sum(d_forget * cell_prev, 1),
                    jnp.sum(d_out * cell_new, 1),
                ]
            )
            param_acc = param_acc + jnp.concatenate([jnp.sum(d_pre, 2), peeps], 0)
            d_low = d_pre.reshape(4 * share, pixels).astype(jnp.bfloat16)
            inp = jnp.concatenate([frame, hidden_in], 0)
            terms = []
            for tap, off in enumerate(offsets):
                moved = tap_shift(inp, off) * masks[tap]
                terms.append(
                    lax.dot_general(d_low, moved, contract_pix, preferred_element_type=jnp.float32)
                )
            weight_acc = weight_acc + jnp.stack(terms, 1)
            everyone = lax.all_gather(d_low, "gate", axis=0, tiled=True)
            ordered = everyone.reshape(groups, 4, share, pixels).transpose(1, 0, 2, 3)
            ordered = ordered.reshape(4 * wide, pixels)
            cols_l = own_cols[layer]
            hidden_back = jnp.zeros((share, pixels), jnp.float32)
            for tap, off in enumerate(offsets):
                part = lax.dot_general(
                    cols_l[:, tap, :], ordered, contract_rows, preferred_element_type=jnp.float32
                )
                hidden_back = hidden_back + tap_shift(part * masks[tap], -off)
            return ((hidden_back, cell_back, grad_head, grad_bias, weight_acc, param_acc), None)

        result, unused = lax.scan(step, carry, stored, reverse=True)
        return result

    zero_hidden = jnp.zeros((wide, pixels), jnp.bfloat16)
    zero_cell = jnp.zeros((share, pixels), jnp.float32)
    (enc_hidden, enc_cell), enc_kept = layer_forward(0, zero_hidden, zero_cell, (frames[:EIN],))
    fore_inputs = (frames[EIN - 1 : EIN + EOUT - 1], frames[EIN:], live)
    unused, fore_kept = layer_forward(1, enc_hidden, enc_cell, fore_inputs)
    error_total = jnp.sum(fore_kept[4])
    fore_prev = jnp.concatenate([enc_hidden[None], fore_kept[2][:-1]], 0)
    fore_stored = (
        fore_kept[0],
        fore_kept[1],
        fore_prev,
        frames[EIN - 1 : EIN + EOUT - 1],
        fore_kept[3],
        fore_kept[2],
    )
    start = (
        zero_cell,
        zero_cell,
        jnp.zeros((chans, wide), jnp.float32),
        jnp.zeros((chans,), jnp.float32),
        jnp.zeros((4 * share, 9, chans + wide), jnp.float32),
        jnp.zeros((7, share), jnp.float32),
    )
    fore_res = layer_backward(1, start, fore_stored)
    enc_prev = jnp.concatenate([zero_hidden[None], enc_kept[2][:-1]], 0)
    enc_stored = (enc_kept[0], enc_kept[1], enc_prev, frames[:EIN])
    enc_start = (fore_res[0], fore_res[1], fore_res[2], fore_res[3], start[4], start[5])
    enc_res = layer_backward(0, enc_start, enc_stored)
    enc_w, enc_p, fore_w, fore_p, grad_head, grad_bias, error_total = lax.psum(
        (enc_res[4], enc_res[5], fore_res[4], fore_res[5], fore_res[2], fore_res[3], error_total),
        "dp",
    )
    grad_conv = jnp.stack([enc_w, fore_w]).reshape(conv_w.shape)
    grad_cell = jnp.stack([enc_p, fore_p])
    loss = error_total / count
    rate = RATE_SCALE * chans * jnp.sqrt(jnp.float32(EOUT * pixels * lax.axis_size("dp")))
    counts_done = step_count.astype(jnp.float32)
    outs = [loss]
    outs += nesterov(conv_w, grad_conv, conv_mom, conv_avg, counts_done[0], rate)
    outs += nesterov(cell_params, grad_cell, cell_mom, cell_avg, counts_done[1], rate)
    outs += nesterov(head_w, grad_head, head_mom, head_avg, counts_done[2], rate)
    outs += nesterov(head_b, grad_bias, bias_mom, bias_avg, counts_done[3], rate)
    return tuple(outs)


def solution(mesh):
    in_specs = (
        P(None, None, "dp"),
        P("dp"),
        P(None, "dp"),
        P(),
        P(None, None, "gate", None),
        P(None, None, "gate"),
        P(),
        P(),
        P(None, None, "gate", None),
        P(None, None, "gate"),
        P(),
        P(),
        P(None, None, "gate", None),
        P(None, None, "gate"),
        P(),
        P(),
    )
    out_specs = (
        P(),
        P(None, None, "gate", None),
        P(None, None, "gate", None),
        P(None, None, "gate", None),
        P(None, None, "gate", None),
        P(None, None, "gate"),
        P(None, None, "gate"),
        P(None, None, "gate"),
        P(None, None, "gate"),
        P(),
        P(),
        P(),
        P(),
        P(),
        P(),
        P(),
        P(),
    )
    return jax.shard_map(
        on_device, mesh=mesh, in_specs=in_specs, out_specs=out_specs, check_vma=False
    )
```

profile of v0, /device:TPU:0, one launch (start us, length us, event | category | flops | bytes accessed | tf_op | source)
XLA Modules:
  0.0 2997.9 jit_solution(8789179289977335016)
XLA Ops:
  24.8 308.2 %while.90 = (s32[]{:T(128)}, bf16[128,4096]{1,0:T(8,128)(2,1)S(1)}, f32[16,4096]{1,0:T(8,128)S(1)}, f32[5,4,16,4096]{3,2,1,0:T(8,128)}, f32[5,16,4096]{2,1,0:T(8...) while((s32[]{:T(128)}, bf16[128,4096]{1,0:T(8,128)(2,1)S(1)}, ...), condition=%wide.region_1.2_spmd.clone, body=%wide.region_0.1_spmd.clone.sunk | while | flops 734265344 | bytes 98123296 | solution.py:104
  45.2 42.0 %all-gather.10.cloned.1.call-done = bf16[128,4096]{1,0:T(8,128)(2,1)} async-done(((bf16[16,4096]{1,0:T(8,128)(2,1)}), bf16[128,4096]{1,0:T(8,128)(2,1)}) %all-gather.10.cloned.1.call-update) | async-done | bytes 1048592 | tf_op jit(solution)/shard_map/while/body/eval_jaxpr/all_gather | solution.py:92
  110.0 38.0 %all-gather.10.cloned.1.call-done = bf16[128,4096]{1,0:T(8,128)(2,1)} async-done(((bf16[16,4096]{1,0:T(8,128)(2,1)}), bf16[128,4096]{1,0:T(8,128)(2,1)}) %all-gather.10.cloned.1.call-update) | async-done | bytes 1048592 | tf_op jit(solution)/shard_map/while/body/eval_jaxpr/all_gather | solution.py:92
  170.8 38.0 %all-gather.10.cloned.1.call-done = bf16[128,4096]{1,0:T(8,128)(2,1)} async-done(((bf16[16,4096]{1,0:T(8,128)(2,1)}), bf16[128,4096]{1,0:T(8,128)(2,1)}) %all-gather.10.cloned.1.call-update) | async-done | bytes 1048592 | tf_op jit(solution)/shard_map/while/body/eval_jaxpr/all_gather | solution.py:92
  231.7 38.0 %all-gather.10.cloned.1.call-done = bf16[128,4096]{1,0:T(8,128)(2,1)} async-done(((bf16[16,4096]{1,0:T(8,128)(2,1)}), bf16[128,4096]{1,0:T(8,128)(2,1)}) %all-gather.10.cloned.1.call-update) | async-done | bytes 1048592 | tf_op jit(solution)/shard_map/while/body/eval_jaxpr/all_gather | solution.py:92
  292.5 38.0 %all-gather.10.cloned.1.call-done = bf16[128,4096]{1,0:T(8,128)(2,1)} async-done(((bf16[16,4096]{1,0:T(8,128)(2,1)}), bf16[128,4096]{1,0:T(8,128)(2,1)}) %all-gather.10.cloned.1.call-update) | async-done | bytes 1048592 | tf_op jit(solution)/shard_map/while/body/eval_jaxpr/all_gather | solution.py:92
  344.0 801.8 %while.89 = (s32[]{:T(128)}, bf16[128,4096]{1,0:T(8,128)(2,1)S(1)}, f32[16,4096]{1,0:T(8,128)S(1)}, f32[15,4,16,4096]{3,2,1,0:T(8,128)}, f32[15,16,4096]{2,1,0:T...) while((s32[]{:T(128)}, bf16[128,4096]{1,0:T(8,128)(2,1)S(1)}, ...), condition=%wide.region_6.7_spmd, body=%wide.region_4.6_spmd.sunk | while | flops 751501312 | bytes 66476440 | solution.py:104
  355.6 37.4 %all-gather.8.cloned.1.call-done = bf16[128,4096]{1,0:T(8,128)(2,1)} async-done(((bf16[16,4096]{1,0:T(8,128)(2,1)}), bf16[128,4096]{1,0:T(8,128)(2,1)}) %all-gather.8.cloned.1.call-update) | async-done | bytes 1048592 | tf_op jit(solution)/shard_map/while/body/eval_jaxpr/all_gather | solution.py:92
  409.3 37.1 %all-gather.8.cloned.1.call-done = bf16[128,4096]{1,0:T(8,128)(2,1)} async-done(((bf16[16,4096]{1,0:T(8,128)(2,1)}), bf16[128,4096]{1,0:T(8,128)(2,1)}) %all-gather.8.cloned.1.call-update) | async-done | bytes 1048592 | tf_op jit(solution)/shard_map/while/body/eval_jaxpr/all_gather | solution.py:92
  462.8 37.1 %all-gather.8.cloned.1.call-done = bf16[128,4096]{1,0:T(8,128)(2,1)} async-done(((bf16[16,4096]{1,0:T(8,128)(2,1)}), bf16[128,4096]{1,0:T(8,128)(2,1)}) %all-gather.8.cloned.1.call-update) | async-done | bytes 1048592 | tf_op jit(solution)/shard_map/while/body/eval_jaxpr/all_gather | solution.py:92
  516.1 37.1 %all-gather.8.cloned.1.call-done = bf16[128,4096]{1,0:T(8,128)(2,1)} async-done(((bf16[16,4096]{1,0:T(8,128)(2,1)}), bf16[128,4096]{1,0:T(8,128)(2,1)}) %all-gather.8.cloned.1.call-update) | async-done | bytes 1048592 | tf_op jit(solution)/shard_map/while/body/eval_jaxpr/all_gather | solution.py:92
  569.6 37.1 %all-gather.8.cloned.1.call-done = bf16[128,4096]{1,0:T(8,128)(2,1)} async-done(((bf16[16,4096]{1,0:T(8,128)(2,1)}), bf16[128,4096]{1,0:T(8,128)(2,1)}) %all-gather.8.cloned.1.call-update) | async-done | bytes 1048592 | tf_op jit(solution)/shard_map/while/body/eval_jaxpr/all_gather | solution.py:92
  623.0 37.1 %all-gather.8.cloned.1.call-done = bf16[128,4096]{1,0:T(8,128)(2,1)} async-done(((bf16[16,4096]{1,0:T(8,128)(2,1)}), bf16[128,4096]{1,0:T(8,128)(2,1)}) %all-gather.8.cloned.1.call-update) | async-done | bytes 1048592 | tf_op jit(solution)/shard_map/while/body/eval_jaxpr/all_gather | solution.py:92
  676.5 37.1 %all-gather.8.cloned.1.call-done = bf16[128,4096]{1,0:T(8,128)(2,1)} async-done(((bf16[16,4096]{1,0:T(8,128)(2,1)}), bf16[128,4096]{1,0:T(8,128)(2,1)}) %all-gather.8.cloned.1.call-update) | async-done | bytes 1048592 | tf_op jit(solution)/shard_map/while/body/eval_jaxpr/all_gather | solution.py:92
  730.0 37.0 %all-gather.8.cloned.1.call-done = bf16[128,4096]{1,0:T(8,128)(2,1)} async-done(((bf16[16,4096]{1,0:T(8,128)(2,1)}), bf16[128,4096]{1,0:T(8,128)(2,1)}) %all-gather.8.cloned.1.call-update) | async-done | bytes 1048592 | tf_op jit(solution)/shard_map/while/body/eval_jaxpr/all_gather | solution.py:92
  783.4 37.0 %all-gather.8.cloned.1.call-done = bf16[128,4096]{1,0:T(8,128)(2,1)} async-done(((bf16[16,4096]{1,0:T(8,128)(2,1)}), bf16[128,4096]{1,0:T(8,128)(2,1)}) %all-gather.8.cloned.1.call-update) | async-done | bytes 1048592 | tf_op jit(solution)/shard_map/while/body/eval_jaxpr/all_gather | solution.py:92
  836.8 37.1 %all-gather.8.cloned.1.call-done = bf16[128,4096]{1,0:T(8,128)(2,1)} async-done(((bf16[16,4096]{1,0:T(8,128)(2,1)}), bf16[128,4096]{1,0:T(8,128)(2,1)}) %all-gather.8.cloned.1.call-update) | async-done | bytes 1048592 | tf_op jit(solution)/shard_map/while/body/eval_jaxpr/all_gather | solution.py:92
  890.3 37.1 %all-gather.8.cloned.1.call-done = bf16[128,4096]{1,0:T(8,128)(2,1)} async-done(((bf16[16,4096]{1,0:T(8,128)(2,1)}), bf16[128,4096]{1,0:T(8,128)(2,1)}) %all-gather.8.cloned.1.call-update) | async-done | bytes 1048592 | tf_op jit(solution)/shard_map/while/body/eval_jaxpr/all_gather | solution.py:92
  943.7 37.1 %all-gather.8.cloned.1.call-done = bf16[128,4096]{1,0:T(8,128)(2,1)} async-done(((bf16[16,4096]{1,0:T(8,128)(2,1)}), bf16[128,4096]{1,0:T(8,128)(2,1)}) %all-gather.8.cloned.1.call-update) | async-done | bytes 1048592 | tf_op jit(solution)/shard_map/while/body/eval_jaxpr/all_gather | solution.py:92
  997.2 37.1 %all-gather.8.cloned.1.call-done = bf16[128,4096]{1,0:T(8,128)(2,1)} async-done(((bf16[16,4096]{1,0:T(8,128)(2,1)}), bf16[128,4096]{1,0:T(8,128)(2,1)}) %all-gather.8.cloned.1.call-update) | async-done | bytes 1048592 | tf_op jit(solution)/shard_map/while/body/eval_jaxpr/all_gather | solution.py:92
  1050.6 37.1 %all-gather.8.cloned.1.call-done = bf16[128,4096]{1,0:T(8,128)(2,1)} async-done(((bf16[16,4096]{1,0:T(8,128)(2,1)}), bf16[128,4096]{1,0:T(8,128)(2,1)}) %all-gather.8.cloned.1.call-update) | async-done | bytes 1048592 | tf_op jit(solution)/shard_map/while/body/eval_jaxpr/all_gather | solution.py:92
  1104.0 37.1 %all-gather.8.cloned.1.call-done = bf16[128,4096]{1,0:T(8,128)(2,1)} async-done(((bf16[16,4096]{1,0:T(8,128)(2,1)}), bf16[128,4096]{1,0:T(8,128)(2,1)}) %all-gather.8.cloned.1.call-update) | async-done | bytes 1048592 | tf_op jit(solution)/shard_map/while/body/eval_jaxpr/all_gather | solution.py:92
  1146.4 13.4 slice.1576
  1169.0 13.1 pad_maximum_fusion.6
  1182.1 22.7 all-gather.6.cloned.1.call-done
  1217.1 1286.9 %while.91 = (s32[]{:T(128)}, f32[16,4096]{1,0:T(8,128)S(1)}, f32[16,4096]{1,0:T(8,128)S(1)}, f32[16,128]{1,0:T(8,128)S(1)}, f32[16]{0:T(128)S(1)}, /*index=5*/f3...) while((s32[]{:T(128)}, f32[16,4096]{1,0:T(8,128)S(1)}, ...), condition=%wide.region_15.16_spmd.clone, body=%wide.region_9.15_spmd.clone.sunk | while | flops 1361062400 | bytes 127451584 | solution.py:165
  1234.5 58.9 %all-gather.12.cloned.1.call-done = bf16[512,4096]{1,0:T(8,128)(2,1)} async-done(((bf16[64,4096]{1,0:T(8,128)(2,1)}), bf16[512,4096]{1,0:T(8,128)(2,1)}) %all-gather.12.cloned.1.call-update) | async-done | bytes 4194320 | tf_op jit(solution)/shard_map/while/body/eval_jaxpr/all_gather | solution.py:153
  1320.4 58.8 %all-gather.12.cloned.1.call-done = bf16[512,4096]{1,0:T(8,128)(2,1)} async-done(((bf16[64,4096]{1,0:T(8,128)(2,1)}), bf16[512,4096]{1,0:T(8,128)(2,1)}) %all-gather.12.cloned.1.call-update) | async-done | bytes 4194320 | tf_op jit(solution)/shard_map/while/body/eval_jaxpr/all_gather | solution.py:153
  1406.1 58.8 %all-gather.12.cloned.1.call-done = bf16[512,4096]{1,0:T(8,128)(2,1)} async-done(((bf16[64,4096]{1,0:T(8,128)(2,1)}), bf16[512,4096]{1,0:T(8,128)(2,1)}) %all-gather.12.cloned.1.call-update) | async-done | bytes 4194320 | tf_op jit(solution)/shard_map/while/body/eval_jaxpr/all_gather | solution.py:153
  1491.8 58.8 %all-gather.12.cloned.1.call-done = bf16[512,4096]{1,0:T(8,128)(2,1)} async-done(((bf16[64,4096]{1,0:T(8,128)(2,1)}), bf16[512,4096]{1,0:T(8,128)(2,1)}) %all-gather.12.cloned.1.call-update) | async-done | bytes 4194320 | tf_op jit(solution)/shard_map/while/body/eval_jaxpr/all_gather | solution.py:153
  1577.6 58.8 %all-gather.12.cloned.1.call-done = bf16[512,4096]{1,0:T(8,128)(2,1)} async-done(((bf16[64,4096]{1,0:T(8,128)(2,1)}), bf16[512,4096]{1,0:T(8,128)(2,1)}) %all-gather.12.cloned.1.call-update) | async-done | bytes 4194320 | tf_op jit(solution)/shard_map/while/body/eval_jaxpr/all_gather | solution.py:153
  1663.3 58.8 %all-gather.12.cloned.1.call-done = bf16[512,4096]{1,0:T(8,128)(2,1)} async-done(((bf16[64,4096]{1,0:T(8,128)(2,1)}), bf16[512,4096]{1,0:T(8,128)(2,1)}) %all-gather.12.cloned.1.call-update) | async-done | bytes 4194320 | tf_op jit(solution)/shard_map/while/body/eval_jaxpr/all_gather | solution.py:153
  1749.1 58.8 %all-gather.12.cloned.1.call-done = bf16[512,4096]{1,0:T(8,128)(2,1)} async-done(((bf16[64,4096]{1,0:T(8,128)(2,1)}), bf16[512,4096]{1,0:T(8,128)(2,1)}) %all-gather.12.cloned.1.call-update) | async-done | bytes 4194320 | tf_op jit(solution)/shard_map/while/body/eval_jaxpr/all_gather | solution.py:153
  1834.8 58.8 %all-gather.12.cloned.1.call-done = bf16[512,4096]{1,0:T(8,128)(2,1)} async-done(((bf16[64,4096]{1,0:T(8,128)(2,1)}), bf16[512,4096]{1,0:T(8,128)(2,1)}) %all-gather.12.cloned.1.call-update) | async-done | bytes 4194320 | tf_op jit(solution)/shard_map/while/body/eval_jaxpr/all_gather | solution.py:153
  1920.6 58.8 %all-gather.12.cloned.1.call-done = bf16[512,4096]{1,0:T(8,128)(2,1)} async-done(((bf16[64,4096]{1,0:T(8,128)(2,1)}), bf16[512,4096]{1,0:T(8,128)(2,1)}) %all-gather.12.cloned.1.call-update) | async-done | bytes 4194320 | tf_op jit(solution)/shard_map/while/body/eval_jaxpr/all_gather | solution.py:153
  2006.3 58.8 %all-gather.12.cloned.1.call-done = bf16[512,4096]{1,0:T(8,128)(2,1)} async-done(((bf16[64,4096]{1,0:T(8,128)(2,1)}), bf16[512,4096]{1,0:T(8,128)(2,1)}) %all-gather.12.cloned.1.call-update) | async-done | bytes 4194320 | tf_op jit(solution)/shard_map/while/body/eval_jaxpr/all_gather | solution.py:153
  2092.1 58.8 %all-gather.12.cloned.1.call-done = bf16[512,4096]{1,0:T(8,128)(2,1)} async-done(((bf16[64,4096]{1,0:T(8,128)(2,1)}), bf16[512,4096]{1,0:T(8,128)(2,1)}) %all-gather.12.cloned.1.call-update) | async-done | bytes 4194320 | tf_op jit(solution)/shard_map/while/body/eval_jaxpr/all_gather | solution.py:153
  2177.8 58.8 %all-gather.12.cloned.1.call-done = bf16[512,4096]{1,0:T(8,128)(2,1)} async-done(((bf16[64,4096]{1,0:T(8,128)(2,1)}), bf16[512,4096]{1,0:T(8,128)(2,1)}) %all-gather.12.cloned.1.call-update) | async-done | bytes 4194320 | tf_op jit(solution)/shard_map/while/body/eval_jaxpr/all_gather | solution.py:153
  2263.6 58.8 %all-gather.12.cloned.1.call-done = bf16[512,4096]{1,0:T(8,128)(2,1)} async-done(((bf16[64,4096]{1,0:T(8,128)(2,1)}), bf16[512,4096]{1,0:T(8,128)(2,1)}) %all-gather.12.cloned.1.call-update) | async-done | bytes 4194320 | tf_op jit(solution)/shard_map/while/body/eval_jaxpr/all_gather | solution.py:153
  2349.3 58.8 %all-gather.12.cloned.1.call-done = bf16[512,4096]{1,0:T(8,128)(2,1)} async-done(((bf16[64,4096]{1,0:T(8,128)(2,1)}), bf16[512,4096]{1,0:T(8,128)(2,1)}) %all-gather.12.cloned.1.call-update) | async-done | bytes 4194320 | tf_op jit(solution)/shard_map/while/body/eval_jaxpr/all_gather | solution.py:153
  2435.1 58.8 %all-gather.12.cloned.1.call-done = bf16[512,4096]{1,0:T(8,128)(2,1)} async-done(((bf16[64,4096]{1,0:T(8,128)(2,1)}), bf16[512,4096]{1,0:T(8,128)(2,1)}) %all-gather.12.cloned.1.call-update) | async-done | bytes 4194320 | tf_op jit(solution)/shard_map/while/body/eval_jaxpr/all_gather | solution.py:153
  2504.8 432.3 %while.92 = (s32[]{:T(128)}, f32[16,4096]{1,0:T(8,128)S(1)}, f32[16,4096]{1,0:T(8,128)S(1)}, f32[64,9,144]{2,0,1:T(8,128)S(1)}, f32[7,16]{1,0:T(8,128)S(1)}, /*i...) while((s32[]{:T(128)}, f32[16,4096]{1,0:T(8,128)S(1)}, ...), condition=%wide.region_21.22_spmd.clone, body=%wide.region_16.21_spmd.clone.sunk | while | flops 1341856256 | bytes 125725872 | solution.py:165
  2520.7 60.6 %all-gather.14.cloned.1.call-done = bf16[512,4096]{1,0:T(8,128)(2,1)} async-done(((bf16[64,4096]{1,0:T(8,128)(2,1)}), bf16[512,4096]{1,0:T(8,128)(2,1)}) %all-gather.14.cloned.1.call-update) | async-done | bytes 4194320 | tf_op jit(solution)/shard_map/while/body/eval_jaxpr/all_gather | solution.py:153
  2607.1 60.7 %all-gather.14.cloned.1.call-done = bf16[512,4096]{1,0:T(8,128)(2,1)} async-done(((bf16[64,4096]{1,0:T(8,128)(2,1)}), bf16[512,4096]{1,0:T(8,128)(2,1)}) %all-gather.14.cloned.1.call-update) | async-done | bytes 4194320 | tf_op jit(solution)/shard_map/while/body/eval_jaxpr/all_gather | solution.py:153
  2693.5 60.7 %all-gather.14.cloned.1.call-done = bf16[512,4096]{1,0:T(8,128)(2,1)} async-done(((bf16[64,4096]{1,0:T(8,128)(2,1)}), bf16[512,4096]{1,0:T(8,128)(2,1)}) %all-gather.14.cloned.1.call-update) | async-done | bytes 4194320 | tf_op jit(solution)/shard_map/while/body/eval_jaxpr/all_gather | solution.py:153
  2780.0 60.7 %all-gather.14.cloned.1.call-done = bf16[512,4096]{1,0:T(8,128)(2,1)} async-done(((bf16[64,4096]{1,0:T(8,128)(2,1)}), bf16[512,4096]{1,0:T(8,128)(2,1)}) %all-gather.14.cloned.1.call-update) | async-done | bytes 4194320 | tf_op jit(solution)/shard_map/while/body/eval_jaxpr/all_gather | solution.py:153
  2866.4 60.7 %all-gather.14.cloned.1.call-done = bf16[512,4096]{1,0:T(8,128)(2,1)} async-done(((bf16[64,4096]{1,0:T(8,128)(2,1)}), bf16[512,4096]{1,0:T(8,128)(2,1)}) %all-gather.14.cloned.1.call-update) | async-done | bytes 4194320 | tf_op jit(solution)/shard_map/while/body/eval_jaxpr/all_gather | solution.py:153
  2957.5 27.3 all-reduce.5.cloned.1.call-done
  (2648 shorter events, 951.8 us)
Async XLA Ops:
  24.8 62.4 %all-gather.10.cloned.1.call-start = ((), (), s32[]{:S(2)}) async-start(), calls=%async_computation.3 | async-start | bytes 1179648 | tf_op jit(solution)/shard_map/while/body/eval_jaxpr/all_gather | solution.py:92
  45.1 44.4 %copy-start.9 = (bf16[9,4096]{1,0:T(8,128)(2,1)S(1)}, bf16[9,4096]{1,0:T(8,128)(2,1)}, u32[]{:S(2)}) copy-start(bf16[9,4096]{1,0:T(8,128)(2,1)} %copy-done.8) | copy-start | bytes 221188 | tf_op jit(solution)/shard_map/while
  45.1 44.4 %copy-start.30 = (bf16[5,16,4096]{2,1,0:T(8,128)(2,1)S(1)}, bf16[5,16,4096]{2,1,0:T(8,128)(2,1)}, u32[]{:S(2)}) copy-start(bf16[5,16,4096]{2,1,0:T(8,128)(2,1)} %copy-done.29) | copy-start | bytes 1966084 | tf_op jit(solution)/shard_map/while
  89.6 58.4 %all-gather.10.cloned.1.call-start = ((), (), s32[]{:S(2)}) async-start(), calls=%async_computation.3 | async-start | bytes 1179648 | tf_op jit(solution)/shard_map/while/body/eval_jaxpr/all_gather | solution.py:92
  150.4 58.4 %all-gather.10.cloned.1.call-start = ((), (), s32[]{:S(2)}) async-start(), calls=%async_computation.3 | async-start | bytes 1179648 | tf_op jit(solution)/shard_map/while/body/eval_jaxpr/all_gather | solution.py:92
  170.8 40.4 %copy-start.9 = (bf16[9,4096]{1,0:T(8,128)(2,1)S(1)}, bf16[9,4096]{1,0:T(8,128)(2,1)}, u32[]{:S(2)}) copy-start(bf16[9,4096]{1,0:T(8,128)(2,1)} %copy-done.8) | copy-start | bytes 221188 | tf_op jit(solution)/shard_map/while
  170.8 40.4 %copy-start.30 = (bf16[5,16,4096]{2,1,0:T(8,128)(2,1)S(1)}, bf16[5,16,4096]{2,1,0:T(8,128)(2,1)}, u32[]{:S(2)}) copy-start(bf16[5,16,4096]{2,1,0:T(8,128)(2,1)} %copy-done.29) | copy-start | bytes 1966084 | tf_op jit(solution)/shard_map/while
  211.3 58.4 %all-gather.10.cloned.1.call-start = ((), (), s32[]{:S(2)}) async-start(), calls=%async_computation.3 | async-start | bytes 1179648 | tf_op jit(solution)/shard_map/while/body/eval_jaxpr/all_gather | solution.py:92
  272.1 58.4 %all-gather.10.cloned.1.call-start = ((), (), s32[]{:S(2)}) async-start(), calls=%async_computation.3 | async-start | bytes 1179648 | tf_op jit(solution)/shard_map/while/body/eval_jaxpr/all_gather | solution.py:92
  344.0 49.0 %all-gather.8.cloned.1.call-start = ((), (), s32[]{:S(2)}) async-start(), calls=%async_computation.2 | async-start | bytes 1179648 | tf_op jit(solution)/shard_map/while/body/eval_jaxpr/all_gather | solution.py:92
  397.7 48.7 %all-gather.8.cloned.1.call-start = ((), (), s32[]{:S(2)}) async-start(), calls=%async_computation.2 | async-start | bytes 1179648 | tf_op jit(solution)/shard_map/while/body/eval_jaxpr/all_gather | solution.py:92
  451.1 48.7 %all-gather.8.cloned.1.call-start = ((), (), s32[]{:S(2)}) async-start(), calls=%async_computation.2 | async-start | bytes 1179648 | tf_op jit(solution)/shard_map/while/body/eval_jaxpr/all_gather | solution.py:92
  504.5 48.7 %all-gather.8.cloned.1.call-start = ((), (), s32[]{:S(2)}) async-start(), calls=%async_computation.2 | async-start | bytes 1179648 | tf_op jit(solution)/shard_map/while/body/eval_jaxpr/all_gather | solution.py:92
  558.0 48.7 %all-gather.8.cloned.1.call-start = ((), (), s32[]{:S(2)}) async-start(), calls=%async_computation.2 | async-start | bytes 1179648 | tf_op jit(solution)/shard_map/while/body/eval_jaxpr/all_gather | solution.py:92
  611.4 48.7 %all-gather.8.cloned.1.call-start = ((), (), s32[]{:S(2)}) async-start(), calls=%async_computation.2 | async-start | bytes 1179648 | tf_op jit(solution)/shard_map/while/body/eval_jaxpr/all_gather | solution.py:92
  664.9 48.7 %all-gather.8.cloned.1.call-start = ((), (), s32[]{:S(2)}) async-start(), calls=%async_computation.2 | async-start | bytes 1179648 | tf_op jit(solution)/shard_map/while/body/eval_jaxpr/all_gather | solution.py:92
  718.3 48.7 %all-gather.8.cloned.1.call-start = ((), (), s32[]{:S(2)}) async-start(), calls=%async_computation.2 | async-start | bytes 1179648 | tf_op jit(solution)/shard_map/while/body/eval_jaxpr/all_gather | solution.py:92
  771.7 48.7 %all-gather.8.cloned.1.call-start = ((), (), s32[]{:S(2)}) async-start(), calls=%async_computation.2 | async-start | bytes 1179648 | tf_op jit(solution)/shard_map/while/body/eval_jaxpr/all_gather | solution.py:92
  825.2 48.7 %all-gather.8.cloned.1.call-start = ((), (), s32[]{:S(2)}) async-start(), calls=%async_computation.2 | async-start | bytes 1179648 | tf_op jit(solution)/shard_map/while/body/eval_jaxpr/all_gather | solution.py:92
  878.7 48.7 %all-gather.8.cloned.1.call-start = ((), (), s32[]{:S(2)}) async-start(), calls=%async_computation.2 | async-start | bytes 1179648 | tf_op jit(solution)/shard_map/while/body/eval_jaxpr/all_gather | solution.py:92
  932.1 48.7 %all-gather.8.cloned.1.call-start = ((), (), s32[]{:S(2)}) async-start(), calls=%async_computation.2 | async-start | bytes 1179648 | tf_op jit(solution)/shard_map/while/body/eval_jaxpr/all_gather | solution.py:92
  985.5 48.7 %all-gather.8.cloned.1.call-start = ((), (), s32[]{:S(2)}) async-start(), calls=%async_computation.2 | async-start | bytes 1179648 | tf_op jit(solution)/shard_map/while/body/eval_jaxpr/all_gather | solution.py:92
  1039.0 48.7 %all-gather.8.cloned.1.call-start = ((), (), s32[]{:S(2)}) async-start(), calls=%async_computation.2 | async-start | bytes 1179648 | tf_op jit(solution)/shard_map/while/body/eval_jaxpr/all_gather | solution.py:92
  1092.4 48.7 %all-gather.8.cloned.1.call-start = ((), (), s32[]{:S(2)}) async-start(), calls=%async_computation.2 | async-start | bytes 1179648 | tf_op jit(solution)/shard_map/while/body/eval_jaxpr/all_gather | solution.py:92
  1145.8 59.1 %all-gather.6.cloned.1.call-start = ((), (), s32[]{:S(2)}) async-start(), calls=%async_computation | async-start | bytes 3244032 | tf_op jit(solution)/shard_map/all_gather | solution.py:62
  1217.0 1287.0 %copy-start.26 = (f32[64,9,144]{2,0,1:T(8,128)S(1)}, f32[64,9,144]{2,0,1:T(8,128)}, u32[]{:S(2)}) copy-start(f32[64,9,144]{2,0,1:T(8,128)} %custom-call.7) | copy-start | bytes 995332
  1217.1 1287.0 %copy-start.43 = (f32[7,16]{1,0:T(8,128)S(1)}, f32[7,16]{1,0:T(8,128)}, u32[]{:S(2)}) copy-start(f32[7,16]{1,0:T(8,128)} %custom-call.8) | copy-start | bytes 1348
  1217.5 76.0 %all-gather.12.cloned.1.call-start = ((), (), s32[]{:S(2)}) async-start(), calls=%async_computation.4 | async-start | bytes 4718592 | tf_op jit(solution)/shard_map/while/body/eval_jaxpr/all_gather | solution.py:153
  1303.3 75.9 %all-gather.12.cloned.1.call-start = ((), (), s32[]{:S(2)}) async-start(), calls=%async_computation.4 | async-start | bytes 4718592 | tf_op jit(solution)/shard_map/while/body/eval_jaxpr/all_gather | solution.py:153
  1389.0 75.9 %all-gather.12.cloned.1.call-start = ((), (), s32[]{:S(2)}) async-start(), calls=%async_computation.4 | async-start | bytes 4718592 | tf_op jit(solution)/shard_map/while/body/eval_jaxpr/all_gather | solution.py:153
  1474.8 75.9 %all-gather.12.cloned.1.call-start = ((), (), s32[]{:S(2)}) async-start(), calls=%async_computation.4 | async-start | bytes 4718592 | tf_op jit(solution)/shard_map/while/body/eval_jaxpr/all_gather | solution.py:153
  1560.5 75.9 %all-gather.12.cloned.1.call-start = ((), (), s32[]{:S(2)}) async-start(), calls=%async_computation.4 | async-start | bytes 4718592 | tf_op jit(solution)/shard_map/while/body/eval_jaxpr/all_gather | solution.py:153
  1646.3 75.9 %all-gather.12.cloned.1.call-start = ((), (), s32[]{:S(2)}) async-start(), calls=%async_computation.4 | async-start | bytes 4718592 | tf_op jit(solution)/shard_map/while/body/eval_jaxpr/all_gather | solution.py:153
  1732.0 75.9 %all-gather.12.cloned.1.call-start = ((), (), s32[]{:S(2)}) async-start(), calls=%async_computation.4 | async-start | bytes 4718592 | tf_op jit(solution)/shard_map/while/body/eval_jaxpr/all_gather | solution.py:153
  1817.8 75.9 %all-gather.12.cloned.1.call-start = ((), (), s32[]{:S(2)}) async-start(), calls=%async_computation.4 | async-start | bytes 4718592 | tf_op jit(solution)/shard_map/while/body/eval_jaxpr/all_gather | solution.py:153
  1903.5 75.9 %all-gather.12.cloned.1.call-start = ((), (), s32[]{:S(2)}) async-start(), calls=%async_computation.4 | async-start | bytes 4718592 | tf_op jit(solution)/shard_map/while/body/eval_jaxpr/all_gather | solution.py:153
  1989.3 75.9 %all-gather.12.cloned.1.call-start = ((), (), s32[]{:S(2)}) async-start(), calls=%async_computation.4 | async-start | bytes 4718592 | tf_op jit(solution)/shard_map/while/body/eval_jaxpr/all_gather | solution.py:153
  2075.0 75.9 %all-gather.12.cloned.1.call-start = ((), (), s32[]{:S(2)}) async-start(), calls=%async_computation.4 | async-start | bytes 4718592 | tf_op jit(solution)/shard_map/while/body/eval_jaxpr/all_gather | solution.py:153
  2160.8 75.9 %all-gather.12.cloned.1.call-start = ((), (), s32[]{:S(2)}) async-start(), calls=%async_computation.4 | async-start | bytes 4718592 | tf_op jit(solution)/shard_map/while/body/eval_jaxpr/all_gather | solution.py:153
  2246.5 75.9 %all-gather.12.cloned.1.call-start = ((), (), s32[]{:S(2)}) async-start(), calls=%async_computation.4 | async-start | bytes 4718592 | tf_op jit(solution)/shard_map/while/body/eval_jaxpr/all_gather | solution.py:153
  2332.3 75.9 %all-gather.12.cloned.1.call-start = ((), (), s32[]{:S(2)}) async-start(), calls=%async_computation.4 | async-start | bytes 4718592 | tf_op jit(solution)/shard_map/while/body/eval_jaxpr/all_gather | solution.py:153
  2418.0 75.9 %all-gather.12.cloned.1.call-start = ((), (), s32[]{:S(2)}) async-start(), calls=%async_computation.4 | async-start | bytes 4718592 | tf_op jit(solution)/shard_map/while/body/eval_jaxpr/all_gather | solution.py:153
  2504.8 76.6 %all-gather.14.cloned.1.call-start = ((), (), s32[]{:S(2)}) async-start(), calls=%async_computation.5 | async-start | bytes 4718592 | tf_op jit(solution)/shard_map/while/body/eval_jaxpr/all_gather | solution.py:153
  2591.2 76.6 %all-gather.14.cloned.1.call-start = ((), (), s32[]{:S(2)}) async-start(), calls=%async_computation.5 | async-start | bytes 4718592 | tf_op jit(solution)/shard_map/while/body/eval_jaxpr/all_gather | solution.py:153
  2677.6 76.6 %all-gather.14.cloned.1.call-start = ((), (), s32[]{:S(2)}) async-start(), calls=%async_computation.5 | async-start | bytes 4718592 | tf_op jit(solution)/shard_map/while/body/eval_jaxpr/all_gather | solution.py:153
  2764.1 76.6 %all-gather.14.cloned.1.call-start = ((), (), s32[]{:S(2)}) async-start(), calls=%async_computation.5 | async-start | bytes 4718592 | tf_op jit(solution)/shard_map/while/body/eval_jaxpr/all_gather | solution.py:153
  2850.5 76.6 %all-gather.14.cloned.1.call-start = ((), (), s32[]{:S(2)}) async-start(), calls=%async_computation.5 | async-start | bytes 4718592 | tf_op jit(solution)/shard_map/while/body/eval_jaxpr/all_gather | solution.py:153
  2937.1 47.6 %all-reduce.5.cloned.1.call-start = ((), (), s32[]{:S(2)}) async-start(), calls=%async_computation.1 | async-start | bytes 1441792 | tf_op jit(solution)/shard_map/psum | solution.py:196
  (400 other events, 902.1 us)
Sparse Core Ops, SparseCore 0:
  44.1 42.9 all-gather.9
  108.9 38.9 all-gather.9
  169.8 38.9 all-gather.9
  230.7 38.9 all-gather.9
  291.5 38.9 all-gather.9
  353.7 39.2 all-gather.7
  407.4 38.9 all-gather.7
  460.8 38.9 all-gather.7
  514.2 38.9 all-gather.7
  567.7 38.9 all-gather.7
  621.1 38.9 all-gather.7
  674.6 38.9 all-gather.7
  728.0 38.9 all-gather.7
  781.4 38.9 all-gather.7
  834.9 38.9 all-gather.7
  888.3 38.9 all-gather.7
  941.8 38.9 all-gather.7
  995.2 38.9 all-gather.7
  1048.6 38.9 all-gather.7
  1102.0 38.9 all-gather.7
  1222.0 71.3 all-gather.11
  1307.8 71.3 all-gather.11
  1393.6 71.3 all-gather.11
  1479.3 71.3 all-gather.11
  1565.1 71.3 all-gather.11
  1650.8 71.3 all-gather.11
  1736.6 71.3 all-gather.11
  1822.3 71.3 all-gather.11
  1908.1 71.3 all-gather.11
  1993.8 71.3 all-gather.11
  2079.6 71.3 all-gather.11
  2165.3 71.3 all-gather.11
  2251.1 71.3 all-gather.11
  2336.8 71.3 all-gather.11
  2422.6 71.3 all-gather.11
  2509.9 71.3 all-gather.13
  2596.3 71.3 all-gather.13
  2682.8 71.3 all-gather.13
  2769.2 71.3 all-gather.13
  2855.6 71.3 all-gather.13
Sparse Core Ops, SparseCore 1:
  1149.0 55.8 all-gather.5
  2951.5 33.2 all-reduce.4
where the time goes:
time: 3010 us; the launch traced here: 3000 us
  waiting for transfers between devices  1990 us (66%)
  matrix products  410 us (14%)
  local copies, waits for them, and re-layouts  306 us (10%)
  other arithmetic  242 us (8%)
    all_gather x20, waiting for transfers between devices, step(): everyone = lax.all_gather(d_low, 'gate', axis=0, tiled=True)  1190 us
    all_gather x20, waiting for transfers between devices, step(): gathered = lax.all_gather(out_slice, 'gate', axis=0, tiled=True)  750 us
    dot_general x180, matrix products, step(): lax.dot_general(cols_l[:, tap, :], ordered, contract_rows, preferred_elem...  122 us
    dot_general x180, matrix products, step(): lax.dot_general(d_low, moved, contract_pix, preferred_element_type=jnp.fl...  104 us
    dot_general x180, matrix products, conv_apply(): jnp.dot(weights_l[:, tap, :], tap_shift(inp, off) * masks[tap], preferred...  95.4 us
    concatenate x160, other arithmetic, step(): inp = jnp.concatenate([xs[0], hidden], 0)  62.1 us
  transfers between devices with their start and end apart: 42, of which 42 were waited for; matrix products, arithmetic and copies ran while one was open for 10% of the time, Pallas kernels for 0%

commit v1 on v0

v1 whole, which is shorter than its diff:
```python
import functools

import jax
import jax.numpy as jnp
from jax import lax
from jax.experimental import pallas as pl
from jax.experimental.pallas import tpu as pltpu
from jax.sharding import PartitionSpec as P

EIN = 5
EOUT = 15
COLS = 128

MU = 0.9
RATE_SCALE = 0.05
F32 = jnp.float32
BF16 = jnp.bfloat16
VMEM_LIMIT = 60 * 1024 * 1024


def ring_order(groups):
    wide = groups // 4
    if wide <= 1:
        return list(range(groups))
    order = [(z, 0) for z in range(4)]
    for z in range(3, -1, -1):
        ys = range(1, wide) if z % 2 else range(wide - 1, 0, -1)
        order += [(z, y) for y in ys]
    return [z * wide + y for z, y in order]


def split_steps(steps, most):
    calls = -(-steps // most)
    base, extra = divmod(steps, calls)
    return [base + (1 if i < extra else 0) for i in range(calls)]


def nesterov(param, grad, mom, avg, steps_done, rate):
    mom_new = MU * mom + grad
    param_new = param - rate * (grad + MU * mom_new)
    avg_new = avg + (param_new - avg) / (steps_done + 1.0)
    return [mom_new, avg_new, param_new, param_new.astype(BF16)]


def logistic(v):
    return 0.5 * jnp.tanh(0.5 * v) + 0.5


def dot_nt(a, b):
    return lax.dot_general(a, b, (((1,), (1,)), ((), ())), preferred_element_type=F32)


def dot_tn(a, b):
    return lax.dot_general(a, b, (((0,), (0,)), ((), ())), preferred_element_type=F32)


def cut(total, pieces):
    base, extra = divmod(total, pieces)
    spans, at = [], 0
    for i in range(pieces):
        size = base + (1 if i < extra else 0)
        spans.append((at, size))
        at += size
    return spans


class Geometry:
    def __init__(self, groups, pixels):
        self.rows = pixels // COLS
        self.own = COLS // groups
        self.halo = min(5, self.own // 2)
        self.calls = [(0, n) for n in split_steps(EIN, self.halo)] + [(1, n) for n in split_steps(EOUT, self.halo)]
        self.front = self.own + 4 * self.halo
        self.back = self.own + 2 * self.halo
        self.union = self.front + (len(self.calls) - 1) * self.halo


def make_variants(geo, hn, hb, mrm, mrp, base):
    rows = geo.rows
    for c0, cw in cut(geo.front, 4):
        r0, m = c0 * rows, cw * rows
        h = hn[r0 : r0 + m, :]
        up = pltpu.roll(h, 1, 0)
        down = pltpu.roll(h, m - 1, 0)
        g0 = base * rows + r0
        hb[0, r0 : r0 + m, :] = up.astype(BF16) * mrm[g0 : g0 + m, :]
        hb[1, r0 : r0 + m, :] = h.astype(BF16)
        hb[2, r0 : r0 + m, :] = down.astype(BF16) * mrp[g0 : g0 + m, :]


def forward_kernel(geo, layer, base, steps, first, *refs):
    refs = list(refs)
    if not first:
        near, far = refs[:2]
        refs = refs[2:]
    xcol, wh, wx, params, mrm, mrp, mcm, mcp = refs[:8]
    gates_out, cprev_out, hvar_out, hnew_out, xown_out, state_out = refs[8:14]
    hb, hn, cb, xs = refs[14:]
    rows, halo, own, front, back = geo.rows, geo.halo, geo.own, geo.front, geo.back
    step = pl.program_id(0)

    @pl.when(step == 0)
    def _():
        if first:
            hn[...] = jnp.zeros_like(hn)
            cb[...] = jnp.zeros_like(cb)
        else:
            nb = back * rows
            hn[:nb, :] = near[:, :128].astype(F32)
            hn[nb:, :] = far[:, :128].astype(F32)
            cb[:nb, :] = near[:, 128:].astype(F32)
            cb[nb:, :] = far[:, 128:].astype(F32)
        make_variants(geo, hn, hb, mrm, mrp, base)

    s0, sn = (2 * halo - 1) * rows, (own + 2) * rows
    for v in range(3):
        hvar_out[0, v, :, :] = hb[v, s0 : s0 + sn, :]
    cprev_out[0, :, :] = cb[halo * rows : (halo + back) * rows, :].astype(BF16)
    xs[...] = xcol[0].T
    xown_out[0, :, :] = xs[2 * halo * rows : (2 * halo + own) * rows, :]

    for c0, cw in cut(front - 2, 4):
        r0, m = (c0 + 1) * rows, cw * rows
        g0 = base * rows + r0
        parts = []
        for dr in range(3):
            left = hb[dr, r0 - rows : r0 - rows + m, :] * mcm[g0 : g0 + m, :]
            mid = hb[dr, r0 : r0 + m, :]
            right = hb[dr, r0 + rows : r0 + rows + m, :] * mcp[g0 : g0 + m, :]
            parts += [left, mid, right]
        z = dot_nt(jnp.concatenate(parts, 1), wh[...]) + dot_nt(xs[r0 : r0 + m, :], wx[...])
        c = cb[r0 : r0 + m, :]
        gi = logistic(z[:, 0:128] + params[0:1, :] + params[4:5, :] * c)
        gf = logistic(z[:, 128:256] + params[1:2, :] + params[5:6, :] * c)
        gg = jnp.tanh(z[:, 384:512] + params[3:4, :])
        cn = gf * c + gi * gg
        go = logistic(z[:, 256:384] + params[2:3, :] + params[6:7, :] * cn)
        h = go * jnp.tanh(cn)
        cb[r0 : r0 + m, :] = cn
        hn[r0 : r0 + m, :] = h.astype(BF16).astype(F32)
        lo, hi = max(c0 + 1, halo), min(c0 + 1 + cw, halo + back)
        a, b = (lo - c0 - 1) * rows, (hi - c0 - 1) * rows
        o = (lo - halo) * rows
        n = b - a
        if n > 0:
            gates_out[0, o : o + n, 0:128] = gi[a:b].astype(BF16)
            gates_out[0, o : o + n, 128:256] = gf[a:b].astype(BF16)
            gates_out[0, o : o + n, 256:384] = go[a:b].astype(BF16)
            gates_out[0, o : o + n, 384:512] = gg[a:b].astype(BF16)
            hnew_out[0, o : o + n, :] = h[a:b].astype(BF16)

    make_variants(geo, hn, hb, mrm, mrp, base)

    @pl.when(step == steps - 1)
    def _():
        a, b = halo * rows, (halo + back) * rows
        state_out[:, :128] = hn[a:b, :].astype(BF16)
        state_out[:, 128:] = cb[a:b, :].astype(BF16)


def whole(shape):
    return pl.BlockSpec(shape, lambda *_: (0,) * len(shape))


def forward_call(geo, layer, base, start, steps, state, xcol, wh, wx, params, masks):
    rows, own, front, back = geo.rows, geo.own, geo.front, geo.back
    chans9 = xcol.shape[1]
    by_step = lambda *dims: pl.BlockSpec((1,) + dims, lambda t: (t,) + (0,) * len(dims))
    operands = list(state) + [xcol, wh, wx, params] + list(masks)
    in_specs = [whole(s.shape) for s in state]
    in_specs += [by_step(chans9, front * rows)]
    in_specs += [whole(v.shape) for v in operands[len(state) + 1 :]]
    shapes = [
        (steps, back * rows, 512),
        (steps, back * rows, 128),
        (steps, 3, (own + 2) * rows, 128),
        (steps, back * rows, 128),
        (steps, own * rows, chans9),
    ]
    outs = [jax.ShapeDtypeStruct(s, BF16) for s in shapes] + [jax.ShapeDtypeStruct((back * rows, 256), BF16)]
    out_specs = [by_step(*s[1:]) for s in shapes] + [whole((back * rows, 256))]
    px = front * rows
    return pl.pallas_call(
        functools.partial(forward_kernel, geo, layer, base, steps, not state),
        grid=(steps,),
        in_specs=in_specs,
        out_specs=out_specs,
        out_shape=outs,
        scratch_shapes=[
            pltpu.VMEM((3, px, 128), BF16),
            pltpu.VMEM((px, 128), F32),
            pltpu.VMEM((px, 128), F32),
            pltpu.VMEM((px, chans9), BF16),
        ],
        compiler_params=pltpu.CompilerParams(vmem_limit_bytes=VMEM_LIMIT),
        cost_estimate=pl.CostEstimate(
            flops=steps * px * 512 * 1296 * 2, bytes_accessed=8 << 20, transcendentals=steps * px * 640
        ),
        name=f"forward_{base}",
    )(*operands)


def backward_kernel(geo, layer, base, steps, first, last, *refs):
    refs = list(refs)
    if not first:
        local, far = refs[:2]
        refs = refs[2:]
    gates, cprev, wb, params, mrm, mrp, mcm, mcp = refs[:8]
    refs = refs[8:]
    if layer == 1:
        hnew, target, live, head, head_b = refs[:5]
        refs = refs[5:]
    dz_out, sums_out, head_out, carry_out, send_out = refs[:5]
    dh, dc, dzb = refs[5:]
    rows, halo, own, back = geo.rows, geo.halo, geo.own, geo.back
    o0, on = halo * rows, own * rows
    step = pl.program_id(0)

    @pl.when(step == 0)
    def _():
        sums_out[...] = jnp.zeros_like(sums_out)
        head_out[...] = jnp.zeros_like(head_out)
        dzb[...] = jnp.zeros_like(dzb)
        if first:
            dh[...] = jnp.zeros_like(dh)
            dc[...] = jnp.zeros_like(dc)
        else:
            nf = 2 * halo * rows
            dh[:nf, :] = far[:, :128].astype(F32)
            dc[:nf, :] = far[:, 128:].astype(F32)
            dh[nf:, :] = local[:, :128]
            dc[nf:, :] = local[:, 128:]

    if layer == 1:
        guess = dot_nt(head[...], hnew[0]) + head_b[...]
        err = guess - target[0].astype(F32)
        dy = live[0] * err
        low = dy.astype(BF16)
        head_out[:, 0:128] += jnp.dot(low[:, o0 : o0 + on], hnew[0, o0 : o0 + on, :], preferred_element_type=F32)
        own_dy = low[:, o0 : o0 + on].astype(F32)
        head_out[:, 128:129] += jnp.sum(own_dy, 1, keepdims=True)
        head_out[:, 129:130] += jnp.sum((dy * err)[:, o0 : o0 + on], 1, keepdims=True)
        dh[...] += dot_tn(low, head[...])

    for c0, cw in cut(back, 4):
        r0, m = c0 * rows, cw * rows
        span = slice(r0, r0 + m)
        gi = gates[0, span, 0:128].astype(F32)
        gf = gates[0, span, 128:256].astype(F32)
        go = gates[0, span, 256:384].astype(F32)
        gg = gates[0, span, 384:512].astype(F32)
        c = cprev[0, span, :].astype(F32)
        cn = gf * c + gi * gg
        tc = jnp.tanh(cn)
        g = dh[span, :]
        d_o = g * tc * go * (1.0 - go)
        d_c = dc[span, :] + g * go * (1.0 - tc * tc) + d_o * params[6:7, :]
        d_i = d_c * gg * gi * (1.0 - gi)
        d_f = d_c * c * gf * (1.0 - gf)
        d_g = d_c * gi * (1.0 - gg * gg)
        dc[span, :] = d_c * gf + d_i * params[4:5, :] + d_f * params[5:6, :]
        p0 = rows + r0
        for n, d in enumerate((d_i, d_f, d_o, d_g)):
            dzb[p0 : p0 + m, n * 128 : (n + 1) * 128] = d.astype(BF16)
        a = max(r0, o0) - r0
        b = min(r0 + m, o0 + on) - r0
        if b > a:
            for n, d in enumerate((d_i, d_f, d_o, d_g, d_i * c, d_f * c, d_o * cn)):
                part = d[a:b].reshape((b - a) // 8, 8, 128)
                sums_out[n * 8 : (n + 1) * 8, :] += jnp.sum(part, 0)

    dz_out[0, :, :] = dzb[rows + o0 : rows + o0 + on, :]

    @pl.when(step < (steps - 1 if last else steps))
    def _():
        for c0, cw in cut(back, 4):
            r0, m = c0 * rows, cw * rows
            total = None
            g0 = (base + halo) * rows + r0
            for dr in range(3):
                parts = []
                for dc_i in range(3):
                    src = r0 - (dc_i - 1) * rows
                    v = dzb[rows + src : rows + src + m, :]
                    gm = g0 - (dc_i - 1) * rows
                    if dc_i == 0:
                        keep = mcm[gm : gm + m, :]
                    elif dc_i == 2:
                        keep = mcp[gm : gm + m, :]
                    if dc_i != 1:
                        v = v * jnp.concatenate([keep] * 4, 1)
                    parts.append(v)
                acc = jnp.dot(jnp.concatenate(parts, 1), wb[dr], preferred_element_type=F32)
                if dr == 0:
                    acc = acc * mrm[g0 : g0 + m, :].astype(F32)
                    acc = pltpu.roll(acc, m - 1, 0)
                elif dr == 2:
                    acc = acc * mrp[g0 : g0 + m, :].astype(F32)
                    acc = pltpu.roll(acc, 1, 0)
                total = acc if total is None else total + acc
            dh[r0 : r0 + m, :] = total

    @pl.when(step == steps - 1)
    def _():
        carry_out[:, :128] = dh[o0 : o0 + on, :]
        carry_out[:, 128:] = dc[o0 : o0 + on, :]
        ns = 2 * halo * rows
        s0 = o0 + on - ns
        send_out[:, :128] = dh[s0 : s0 + ns, :].astype(BF16)
        send_out[:, 128:] = dc[s0 : s0 + ns, :].astype(BF16)


def backward_call(geo, layer, base, steps, last, state, saved, wb, params, masks, extra):
    rows, own, back, halo = geo.rows, geo.own, geo.back, geo.halo
    by_step = lambda *dims: pl.BlockSpec((1,) + dims, lambda t: (steps - 1 - t,) + (0,) * len(dims))
    operands = list(state) + [saved["gates"], saved["cprev"], wb, params] + list(masks)
    in_specs = [whole(s.shape) for s in state]
    in_specs += [by_step(back * rows, 512), by_step(back * rows, 128)]
    in_specs += [whole(v.shape) for v in operands[len(state) + 2 :]]
    if layer == 1:
        target, live, head, head_b = extra
        operands += [saved["hnew"], target, live, head, head_b]
        in_specs += [
            by_step(back * rows, 128),
            by_step(target.shape[1], back * rows),
            by_step(1, back * rows),
            whole(head.shape),
            whole(head_b.shape),
        ]
    outs = [
        jax.ShapeDtypeStruct((steps, own * rows, 512), BF16),
        jax.ShapeDtypeStruct((56, 128), F32),
        jax.ShapeDtypeStruct((16, 256), F32),
        jax.ShapeDtypeStruct((own * rows, 256), F32),
        jax.ShapeDtypeStruct((2 * halo * rows, 256), BF16),
    ]
    out_specs = [by_step(own * rows, 512)] + [whole(o.shape) for o in outs[1:]]
    px = back * rows
    return pl.pallas_call(
        functools.partial(backward_kernel, geo, layer, base, steps, not state, last),
        grid=(steps,),
        in_specs=in_specs,
        out_specs=out_specs,
        out_shape=outs,
        scratch_shapes=[
            pltpu.VMEM((px, 128), F32),
            pltpu.VMEM((px, 128), F32),
            pltpu.VMEM((px + 2 * rows, 512), BF16),
        ],
        compiler_params=pltpu.CompilerParams(vmem_limit_bytes=VMEM_LIMIT),
        cost_estimate=pl.CostEstimate(
            flops=steps * px * 512 * 1536 * 2, bytes_accessed=8 << 20, transcendentals=steps * px * 128
        ),
        name=f"backward_{base}",
    )(*operands)


def weight_kernel(geo, base, steps, add, *refs):
    if add:
        acc, dz, hvar, xown, mcm, mcp, out, rhs = refs
    else:
        dz, hvar, xown, mcm, mcp, out, rhs = refs
    rows, own, halo = geo.rows, geo.own, geo.halo
    on = own * rows
    g0 = (base + 2 * halo) * rows
    wide = hvar.shape[-1]
    taps = [(dr, dc) for dr in range(3) for dc in range(3)]
    for n in range(0, 10, 2):
        for k in range(2):
            for j in range(steps):
                at = slice(j * on, (j + 1) * on)
                if n + k < 9:
                    dr, dc = taps[n + k]
                    v = hvar[j, dr, dc * rows : dc * rows + on, :]
                    if dc == 0:
                        v = v * mcm[g0 : g0 + on, :]
                    elif dc == 2:
                        v = v * mcp[g0 : g0 + on, :]
                    rhs[at, k * wide : (k + 1) * wide] = v
                else:
                    rhs[at, wide : wide + xown.shape[-1]] = xown[j]
        width = 2 * wide if n + 1 < 9 else wide + xown.shape[-1]
        lo = n * wide
        g = dot_tn(dz[...], rhs[:, :width])
        if add:
            g = g + acc[:, lo : lo + width]
        out[:, lo : lo + width] = g


def weight_call(geo, base, steps, acc, dz, hvar, xown, mcm, mcp):
    on = geo.own * geo.rows
    dz = dz.reshape(steps * on, 512)
    chans9 = xown.shape[-1]
    operands = ([] if acc is None else [acc]) + [dz, hvar, xown, mcm, mcp]
    return pl.pallas_call(
        functools.partial(weight_kernel, geo, base, steps, acc is not None),
        out_shape=jax.ShapeDtypeStruct((512, 1152 + chans9), F32),
        scratch_shapes=[pltpu.VMEM((steps * on, 384), BF16)],
        compiler_params=pltpu.CompilerParams(vmem_limit_bytes=VMEM_LIMIT),
        cost_estimate=pl.CostEstimate(
            flops=steps * on * 512 * 1296 * 2, bytes_accessed=16 << 20, transcendentals=0
        ),
        name=f"weights_{base}",
    )(*operands)


def swap_pairs(size, bit):
    return [(i, i ^ bit) for i in range(size)]


def butterfly_bits(size):
    bits, bit = [], 1
    while bit < size:
        bits.append(bit)
        bit *= 2
    return bits


def gather_dp(piece, ranks):
    me = lax.axis_index("dp")
    for bit in butterfly_bits(ranks)[1:] + [1]:
        other = lax.ppermute(piece, "dp", swap_pairs(ranks, bit))
        high = (me & bit) != 0
        pair = jnp.stack([jnp.where(high, other, piece), jnp.where(high, piece, other)])
        if bit == 1:
            piece = jnp.swapaxes(pair, 0, 1).reshape((-1,) + piece.shape[1:])
        else:
            piece = pair.reshape((-1,) + piece.shape[1:])
    return piece


def scatter_sum_dp(whole_sum, ranks, small):
    me = lax.axis_index("dp")
    value = whole_sum
    bits = butterfly_bits(ranks)
    for n, bit in enumerate([1] + bits[:0:-1]):
        if bit == 1:
            halves = value.reshape((ranks // 2, 2) + value.shape[1:])
            low, high = halves[:, 0], halves[:, 1]
        else:
            half = value.shape[0] // 2
            low, high = value[:half], value[half:]
        mine_high = (me & bit) != 0
        send = jnp.where(mine_high, low, high).astype(BF16)
        keep = jnp.where(mine_high, high, low)
        pairs = swap_pairs(ranks, bit)
        value = keep + lax.ppermute(send, "dp", pairs).astype(F32)
        hi = small.astype(BF16)
        lo = (small - hi.astype(F32)).astype(BF16)
        got = lax.ppermute(jnp.stack([hi, lo]), "dp", pairs).astype(F32)
        small = small + (got[0] + got[1])
    return value[0], small


def on_device(
    frames,
    regions,
    valid,
    step_count,
    conv_w,
    cell_params,
    head_w,
    head_b,
    conv_mom,
    cell_mom,
    head_mom,
    bias_mom,
    conv_avg,
    cell_avg,
    head_avg,
    bias_avg,
):
    share = conv_w.shape[2]
    chans = frames.shape[1]
    pixels = frames.shape[2]
    wide = head_w.shape[1]
    groups = lax.axis_size("gate")
    ranks = lax.axis_size("dp")
    geo = Geometry(groups, pixels)
    rows, own, halo, front, back, union = geo.rows, geo.own, geo.halo, geo.front, geo.back, geo.union
    gate_at = lax.axis_index("gate")
    dp_at = lax.axis_index("dp")

    order = ring_order(groups)
    place = [order.index(g) for g in range(groups)]
    spot = jnp.asarray(place, jnp.int32)[gate_at]
    from_right = [(order[(i + 1) % groups], order[i]) for i in range(groups)]
    from_left = [(order[i], order[(i + 1) % groups]) for i in range(groups)]

    taps = conv_w.reshape(2, 4 * share, 9, chans + wide).astype(BF16)
    packed = jnp.concatenate(
        [taps[..., chans:].reshape(2, 4 * share, 9 * wide), taps[..., :chans].reshape(2, 4 * share, 9 * chans)], -1
    )
    slab = 4 * share // ranks
    packed_w = packed.shape[-1]
    mine = lax.dynamic_slice_in_dim(packed.reshape(2, ranks, slab, packed_w), dp_at, 1, 1)[:, 0]
    everyone = lax.all_to_all(
        jnp.broadcast_to(mine[None], (groups, 2, slab, packed_w)), "gate", 0, 0, tiled=True
    )
    gathered = gather_dp(everyone[None], ranks)
    full = gathered.transpose(2, 1, 0, 3, 4).reshape(2, groups, 4, share, packed_w)
    full = full.transpose(0, 2, 1, 3, 4).reshape(2, 4 * wide, packed_w)
    cell_all = lax.all_gather(cell_params, "gate", axis=2, tiled=True)

    def window(field, dtype):
        lead = field.shape[:-1]
        grid = jnp.swapaxes(field.astype(dtype).reshape(lead + (rows, COLS)), -1, -2)
        flat = grid.reshape(lead + (pixels,))
        start = jnp.mod(spot * own - 2 * halo - 1, COLS) * rows
        twice = jnp.concatenate([flat, flat], -1)
        return lax.dynamic_slice_in_dim(twice, start, (union + 2) * rows, len(lead))

    px = union * rows
    ids = window(regions, jnp.int32)
    pad_ids = jnp.pad(ids, (1, 1), constant_values=-1)
    offsets = [dc * rows + dr for dr in (-1, 0, 1) for dc in (-1, 0, 1)]

    def shifted(v, off):
        return lax.slice_in_dim(v, 1 + rows + off, 1 + rows + off + px, axis=v.ndim - 1)

    here = shifted(pad_ids, 0)
    keeps = [shifted(pad_ids, off) == here for off in offsets]
    spread = lambda m: jnp.broadcast_to(m[:, None], (px, 128)).astype(BF16)
    column_ids = here - here % 2
    pad_cols = pad_ids - pad_ids % 2
    masks = (
        spread(keeps[1]),
        spread(keeps[7]),
        spread(shifted(pad_cols, -rows) == column_ids),
        spread(shifted(pad_cols, rows) == column_ids),
    )
    seen = window(frames, BF16)
    pad_seen = jnp.pad(seen, ((0, 0), (0, 0), (1, 1)))
    xcol = jnp.concatenate(
        [jnp.where(keep, shifted(pad_seen, off), jnp.zeros((), BF16)) for keep, off in zip(keeps, offsets)], 1
    )
    centre = shifted(pad_seen, 0)
    live = shifted(jnp.pad(window(valid, F32), ((0, 0), (1, 1))), 0)[:, None, :]

    head_low = head_w.astype(BF16)
    head_bias = head_b[:, None]
    wh = [full[l, :, : 9 * wide] for l in range(2)]
    wx = [full[l, :, 9 * wide :] for l in range(2)]
    wb = [
        wh[l].reshape(4 * wide, 3, 3, wide).transpose(1, 2, 0, 3).reshape(3, 3 * 4 * wide, wide) for l in range(2)
    ]

    state = ()
    kept = []
    t = 0
    for n, (layer, steps) in enumerate(geo.calls):
        base = n * halo
        first_frame = t if layer == 0 else t - 1
        xin = xcol[first_frame : first_frame + steps, :, base * rows : (base + front) * rows]
        got = forward_call(geo, layer, base, t, steps, state, xin, wh[layer], wx[layer], cell_all[layer], masks)
        kept.append(dict(gates=got[0], cprev=got[1], hvar=got[2], hnew=got[3], xown=got[4], t=t))
        out = got[5]
        t += steps
        if n + 1 < len(geo.calls):
            far = lax.ppermute(out[2 * halo * rows : 4 * halo * rows], "gate", from_right)
            state = (out, far)

    state = ()
    grads = [None, None]
    cell_sums = [jnp.zeros((56, 128), F32) for _ in range(2)]
    head_sums = jnp.zeros((16, 256), F32)
    for n in range(len(geo.calls) - 1, -1, -1):
        layer, steps = geo.calls[n]
        base = n * halo
        saved = kept[n]
        extra = None
        if layer == 1:
            t = saved["t"]
            a, b = (base + halo) * rows, (base + halo + back) * rows
            extra = (centre[t : t + steps, :, a:b], live[t - EIN : t - EIN + steps, :, a:b], head_low, head_bias)
        got = backward_call(
            geo, layer, base, steps, n == 0, state, saved, wb[layer], cell_all[layer], masks, extra
        )
        if n > 0:
            far = lax.ppermute(got[4], "gate", from_left)
            state = (got[3], far)
        grads[layer] = weight_call(
            geo, base, steps, grads[layer], got[0], saved["hvar"], saved["xown"], masks[2], masks[3]
        )
        cell_sums[layer] = cell_sums[layer] + got[1]
        if layer == 1:
            head_sums = head_sums + got[2]

    cells = jnp.stack(cell_sums).reshape(2, 7, 8, wide).sum(2)
    mine_live = lax.dynamic_slice_in_dim(valid.reshape(EOUT, rows, COLS), spot * own, own, 2)
    counted = jnp.sum(mine_live).astype(F32)
    loss_sum = jnp.sum(head_sums[:, 129])
    shared_small = jnp.concatenate(
        [head_sums[:, :128].reshape(-1), head_sums[:, 128], loss_sum[None], counted[None]]
    )
    small = jnp.concatenate([cells.reshape(-1), shared_small])
    big = jnp.stack(grads).reshape(2, 4, groups, share, packed_w).transpose(2, 1, 3, 0, 4)
    big = big.reshape(groups, ranks, slab, 2, packed_w).transpose(1, 0, 2, 3, 4)
    part, small = scatter_sum_dp(big, ranks, small)
    ncell = 14 * wide
    for_gate = small[:ncell].reshape(14, groups, share).transpose(1, 0, 2).reshape(groups, 14 * share)
    to_gate = jnp.concatenate(
        [for_gate, jnp.broadcast_to(small[None, ncell:], (groups, small.shape[0] - ncell))], 1
    )
    hi = to_gate.astype(BF16)
    lo = (to_gate - hi.astype(F32)).astype(BF16)
    width = slab * 2 * packed_w
    message = jnp.concatenate([part.reshape(groups, width).astype(BF16), hi, lo], 1)
    got = lax.all_to_all(message, "gate", 0, 0, tiled=True).astype(F32)
    got = jnp.sum(got.reshape(groups, -1), 0)
    nsmall = to_gate.shape[1]
    small_sum = got[width : width + nsmall] + got[width + nsmall :]
    piece = got[:width].reshape(1, slab, 2, packed_w)
    rows_all = gather_dp(piece, ranks).reshape(4 * share, 2, packed_w).transpose(1, 0, 2)
    count = chans * small_sum[-1]
    scale = 2.0 / count
    rows_all = rows_all * scale
    grad_conv = jnp.concatenate(
        [
            rows_all[..., 9 * wide :].reshape(2, 4 * share, 9, chans),
            rows_all[..., : 9 * wide].reshape(2, 4 * share, 9, wide),
        ],
        -1,
    ).reshape(conv_w.shape)
    grad_cell = small_sum[: 14 * share].reshape(2, 7, share) * scale
    rest = small_sum[14 * share :]
    grad_head = rest[: chans * wide].reshape(chans, wide) * scale
    grad_bias = rest[chans * wide : chans * wide + chans] * scale
    loss = rest[chans * wide + chans] / count

    rate = RATE_SCALE * chans * jnp.sqrt(jnp.float32(EOUT * pixels * ranks))
    counts_done = step_count.astype(F32)
    outs = [loss]
    outs += nesterov(conv_w, grad_conv, conv_mom, conv_avg, counts_done[0], rate)
    outs += nesterov(cell_params, grad_cell, cell_mom, cell_avg, counts_done[1], rate)
    outs += nesterov(head_w, grad_head, head_mom, head_avg, counts_done[2], rate)
    outs += nesterov(head_b, grad_bias, bias_mom, bias_avg, counts_done[3], rate)
    return tuple(outs)


def solution(mesh):
    in_specs = (
        P(None, None, "dp"),
        P("dp"),
        P(None, "dp"),
        P(),
        P(None, None, "gate", None),
        P(None, None, "gate"),
        P(),
        P(),
        P(None, None, "gate", None),
        P(None, None, "gate"),
        P(),
        P(),
        P(None, None, "gate", None),
        P(None, None, "gate"),
        P(),
        P(),
    )
    out_specs = (
        P(),
        P(None, None, "gate", None),
        P(None, None, "gate", None),
        P(None, None, "gate", None),
        P(None, None, "gate", None),
        P(None, None, "gate"),
        P(None, None, "gate"),
        P(None, None, "gate"),
        P(None, None, "gate"),
        P(),
        P(),
        P(),
        P(),
        P(),
        P(),
        P(),
        P(),
    )
    return jax.shard_map(
        on_device, mesh=mesh, in_specs=in_specs, out_specs=out_specs, check_vma=False
    )
```

time: 3010 us -> 433 us (0.14)
  waiting for transfers between devices: 1990 us -> 50.8 us
  matrix products: 410 us -> 0 us
  local copies, waits for them, and re-layouts: 306 us -> 82.3 us
  other arithmetic: 242 us -> 41.9 us
  Pallas kernels: 0 us -> 185 us
    all_gather x41 -> x0, waiting for transfers between devices: 1960 us -> none  [the longest x20 1190 us: step(): everyone = lax.all_gather(d_low, 'gate', axis=0, tiled=True)]
    dot_general x585 -> x0, matrix products: 410 us -> none  [the longest x180 122 us: step(): lax.dot_general(cols_l[:, tap, :], ordered, contract_rows, preferred_elem...]
    pallas_call x0 -> x12, Pallas kernels: none -> 185 us  [the longest x4 78.9 us: backward_call(): pl.pallas_call(functools.partial(backward_kernel, geo, layer, base, steps...]
    concatenate x321 -> x5, other arithmetic: 111 us -> 5.89 us  [the longest x3 2.53 us: window(): twice = jnp.concatenate([flat, flat], -1)]
    squeeze x83 -> x1, local copies, waits for them, and re-layouts: 60.1 us -> 0.82 us  [on_device(): wx = [full[l, :, 9 * wide:] for l in range(2)]]
    dynamic_update_slice x50 -> x0, local copies, waits for them, and re-layouts: 50.2 us -> none  [layer_forward(): return lax.scan(step, (hidden, cell), inputs)]
    reduce_sum x62 -> x4, other arithmetic: 52.3 us -> 4.06 us  [the longest x1 1.85 us: on_device(): got = jnp.sum(got.reshape(groups, -1), 0)]
    slice x514 -> x19, local copies, waits for them, and re-layouts: 66.3 us -> 18.1 us  [the longest x1 8.65 us: on_device(): xcol[first_frame:first_frame + steps, :, base * rows:(base + front) * rows]]
  transfers between devices with their start and end apart: 42 -> 16, of which waited for: 42 -> 7; matrix products, arithmetic and copies ran while one was open for 10% -> 18% of each run, Pallas kernels for 0% -> 9%
where the time goes in v1:
time: 433 us; the launch traced here: 426 us
  Pallas kernels  185 us (43%)
  local copies, waits for them, and re-layouts  82.3 us (19%)
  waiting for transfers between devices  50.8 us (12%)
  other arithmetic  41.9 us (10%)
  blocking collectives  31.2 us (7%)
  starting transfers between devices  27 us (6%)
  between operations  8.29 us (2%)
    pallas_call x4, Pallas kernels, backward_call(): pl.pallas_call(functools.partial(backward_kernel, geo, layer, base, steps...  78.9 us
    pallas_call x4, Pallas kernels, forward_call(): pl.pallas_call(functools.partial(forward_kernel, geo, layer, base, steps,...  66.5 us
    pallas_call x4, Pallas kernels, weight_call(): pl.pallas_call(functools.partial(weight_kernel, geo, base, steps, acc is...  39.5 us
    all_gather x1, blocking collectives, on_device(): cell_all = lax.all_gather(cell_params, 'gate', axis=2, tiled=True)  31.2 us
    unnamed x77, local copies, waits for them, and re-layouts  18.1 us
    reshape x3, local copies, waits for them, and re-layouts, window(): flat = grid.reshape(lead + (pixels,))  16.7 us
    ppermute x2, waiting for transfers between devices, scatter_sum_dp(): value = keep + lax.ppermute(send, 'dp', pairs).astype(F32)  15.4 us
    all_to_all x1, waiting for transfers between devices, on_device(): got = lax.all_to_all(message, 'gate', 0, 0, tiled=True).astype(F32)  14.1 us
  transfers between devices with their start and end apart: 16, of which 7 were waited for; matrix products, arithmetic and copies ran while one was open for 18% of the time, Pallas kernels for 9%

profile of v1, /device:TPU:0, one launch (start us, length us, event | category | flops | bytes accessed | tf_op | source)
XLA Modules:
  0.0 426.3 jit_solution(1282527345213656855)
XLA Ops:
  5.1 7.3 %all-to-all-start = ((bf16[8,2,16,1296]{3,2,1,0:T(8,128)(2,1)}), bf16[8,2,16,1296]{3,2,1,0:T(8,128)(2,1)S(1)}, u32[]{:S(2)}, u32[]{:S(2)}) async-start(bf16[8,2,16,1296]{3,2,1,0:T(8,128)(2,1)} %broadcast_in_dim.100), calls=%async_computation | async-start | bytes 1441792 | tf_op jit(solution)/shard_map/all_to_all | solution.py:497
  14.1 2.3 copy.186
  16.4 7.2 %copy.145 = bf16[20,16,32,128]{2,3,1,0:T(8,128)(2,1)} copy(bf16[20,16,32,128]{3,2,1,0:T(8,128)(2,1)S(1)} %bitcast.155) | data formatting | bytes 5242880 | tf_op jit(solution)/shard_map/reshape | solution.py:507
  23.7 14.2 %reshape.376 = bf16[20,16,4096]{2,1,0:T(8,128)(2,1)} reshape(bf16[20,16,128,32]{3,2,1,0:T(8,128)(2,1)} %bitcast.148) | data formatting | bytes 5242880 | tf_op jit(solution)/shard_map/reshape | solution.py:508
  37.9 2.3 fusion.3
  41.7 1.5 fusion.9
  43.2 1.6 fusion.8
  47.5 31.2 %all_gather.3 = f32[2,7,128]{1,0,2:T(2,128)S(1)} all-gather(f32[2,7,16]{1,0,2:T(2,128)S(1)} %copy.151), channel_id=1, replica_groups=mesh['dp'=4,'gate'=8] {'gate'}, dimensions={2}, use_global_device_ids=true | all-gather | bytes 8064 | tf_op jit(solution)/shard_map/all_gather | solution.py:503
  78.7 1.5 fusion.6
  80.3 1.6 fusion.5
  84.9 8.2 %collective-permute-done = bf16[1,8,2,16,1296]{4,3,2,1,0:T(8,128)(2,1)S(1)} collective-permute-done((bf16[1,8,2,16,1296]{4,3,2,1,0:T(8,128)(2,1)S(1)}, bf16[1,8,2,16,1296]{4,3,2,1,0:T(8,128)(2,1)S(1)}, u32[]{:S(2)}, u32[]{:S(2)}) %collective-permute-start) | collective-permute-done | bytes 663584 | tf_op jit(solution)/shard_map/ppermute | solution.py:422
  100.3 2.4 reshape.382
  104.2 8.6 %fusion.37 = (bf16[5,144,1152]{2,1,0:T(8,128)(2,1)}, bf16[5,144,1152]{2,1,0:T(8,128)(2,1)}, bf16[5,144,1152]{2,1,0:T(8,128)(2,1)}, bf16[5,144,1152]{2,1,0:T(8,128)(2,1)}) fusion(bf16[20,144,1632]{2,1,0:T(8,128)(2,1)} %select_dynamic-update-slice_fusion), kind=kLoop, calls=%fused_computation.127 | loop fusion | bytes 13271040 | tf_op jit(solution)/shard_map/slice | solution.py:554
  112.9 1.7 select_bitcast_fusion.1
  116.0 1.8 fusion.38
  121.9 16.4 %forward_0.1 = (bf16[5,832,512]{2,1,0:T(8,128)(2,1)}, bf16[5,832,128]{2,1,0:T(8,128)(2,1)}, bf16[5,3,576,128]{3,2,1,0:T(8,128)(2,1)}, bf16[5,832,128]{2,1,0:T(8,...) custom-call(bf16[5,144,1152]{2,1,0:T(8,128)(2,1)} %get-tuple-element.185.refs_0_, ...), custom_call_target="tpu_custom_call" | custom-call | flops 7644119040 | bytes 8388608 | tf_op jit(solution)/shard_map/forward_0/pallas_call | solution.py:183
  139.2 1.8 collective-permute-start.2
  141.2 4.9 %collective-permute-done.2.refs_1_ = bf16[320,256]{1,0:T(8,128)(2,1)S(1)} collective-permute-done((bf16[320,256]{1,0:T(8,128)(2,1)S(1)}, bf16[320,256]{1,0:T(8,128)(2,1)S(1)}, u32[]{:S(2)}, u32[]{:S(2)}) %collective-permute-start.2) | collective-permute-done | bytes 163872 | tf_op jit(solution)/shard_map/ppermute | solution.py:560
  146.8 16.7 %forward_5.1 = (bf16[5,832,512]{2,1,0:T(8,128)(2,1)}, bf16[5,832,128]{2,1,0:T(8,128)(2,1)}, bf16[5,3,576,128]{3,2,1,0:T(8,128)(2,1)}, bf16[5,832,128]{2,1,0:T(8,...) custom-call(bf16[832,256]{1,0:T(8,128)(2,1)} %get-tuple-element.56.refs_0_, ...), custom_call_target="tpu_custom_call" | custom-call | flops 7644119040 | bytes 8388608 | tf_op jit(solution)/shard_map/forward_5/pallas_call | solution.py:183
  164.4 1.6 collective-permute-start.3
  166.9 3.4 collective-permute-done.3.refs_1_
  170.9 16.7 %forward_10.1 = (bf16[5,832,512]{2,1,0:T(8,128)(2,1)}, bf16[5,832,128]{2,1,0:T(8,128)(2,1)}, bf16[5,3,576,128]{3,2,1,0:T(8,128)(2,1)}, bf16[5,832,128]{2,1,0:T(8...) custom-call(bf16[832,256]{1,0:T(8,128)(2,1)} %get-tuple-element.57.refs_0_, ...), custom_call_target="tpu_custom_call" | custom-call | flops 7644119040 | bytes 8388608 | tf_op jit(solution)/shard_map/forward_10/pallas_call | solution.py:183
  188.5 1.6 collective-permute-start.4
  192.3 2.4 copy.161
  197.4 16.7 %forward_15.1 = (bf16[5,832,512]{2,1,0:T(8,128)(2,1)}, bf16[5,832,128]{2,1,0:T(8,128)(2,1)}, bf16[5,3,576,128]{3,2,1,0:T(8,128)(2,1)}, bf16[5,832,128]{2,1,0:T(8...) custom-call(bf16[832,256]{1,0:T(8,128)(2,1)} %get-tuple-element.58.refs_0_, ...), custom_call_target="tpu_custom_call" | custom-call | flops 7644119040 | bytes 8388608 | tf_op jit(solution)/shard_map/forward_15/pallas_call | solution.py:183
  214.2 20.4 %backward_15.1 = (bf16[5,512,512]{2,1,0:T(8,128)(2,1)}, f32[56,128]{1,0:T(8,128)}, f32[16,256]{1,0:T(8,128)}, f32[512,256]{1,0:T(8,128)}, bf16[320,256]{1,0:T(8,128)(2,1)}) custom-call(bf16[5,832,512]{2,1,0:T(8,128)(2,1)} %get-tuple-element.59.refs_0_, bf16[5,832,128]{2,1,0:T(8,128)(2,1)} %get-tuple-element.60.refs_1_, bf16[3,1536,128]{2,1,0:T(8,128)(2,1)} %bitcast.168, ...), custom_call_target="tpu_custom_call" | custom-call | flops 6543114240 | bytes 8388608 | tf_op jit(solution)/shard_map/backward_15/pallas_call | solution.py:339
  235.6 9.4 %weights_15.1.refs_0_ = f32[512,1296]{1,0:T(8,128)} custom-call(bf16[2560,512]{1,0:T(8,128)(2,1)} %bitcast.191, bf16[5,3,576,128]{3,2,1,0:T(8,128)(2,1)} %get-tuple-element.80.refs_1_, bf16[5,512,144]{2,1,0:T(8,128)(2,1)} %get-tuple-element.81.refs_2_, bf16[1632,128]{1,0:T(8,128)(2,1)} %broadcast_in_dim.104.refs_6_.refs_8_.refs_3_.refs_4_, ...), custom_call_target="tpu_custom_call" | custom-call | flops 3397386240 | bytes 16777216 | tf_op jit(solution)/shard_map/weights_15/pallas_call | solution.py:395
  245.6 20.6 %backward_10.1 = (bf16[5,512,512]{2,1,0:T(8,128)(2,1)}, f32[56,128]{1,0:T(8,128)}, f32[16,256]{1,0:T(8,128)}, f32[512,256]{1,0:T(8,128)}, bf16[320,256]{1,0:T(8,128)(2,1)}) custom-call(f32[512,256]{1,0:T(8,128)} %get-tuple-element.62.refs_0_, bf16[320,256]{1,0:T(8,128)(2,1)} %copy-done.26, bf16[5,832,512]{2,1,0:T(8,128)(2,1)} %get-tuple-element.64.refs_2_, ...), custom_call_target="tpu_custom_call" | custom-call | flops 6543114240 | bytes 8388608 | tf_op jit(solution)/shard_map/backward_10/pallas_call | solution.py:339
  267.2 10.2 %weights_10.1.refs_0_ = f32[512,1296]{1,0:T(8,128)} custom-call(f32[512,1296]{1,0:T(8,128)} %weights_15.1.refs_0_, bf16[2560,512]{1,0:T(8,128)(2,1)} %bitcast.166, bf16[5,3,576,128]{3,2,1,0:T(8,128)(2,1)} %get-tuple-element.83.refs_2_, bf16[5,512,144]{2,1,0:T(8,128)(2,1)} %get-tuple-element.84.refs_3_, ...), custom_call_target="tpu_custom_call" | custom-call | flops 3397386240 | bytes 16777216 | tf_op jit(solution)/shard_map/weights_10/pallas_call | solution.py:395
  278.1 20.7 %backward_5.1 = (bf16[5,512,512]{2,1,0:T(8,128)(2,1)}, f32[56,128]{1,0:T(8,128)}, f32[16,256]{1,0:T(8,128)}, f32[512,256]{1,0:T(8,128)}, bf16[320,256]{1,0:T(8,128)(2,1)}) custom-call(f32[512,256]{1,0:T(8,128)} %get-tuple-element.67.refs_0_, bf16[320,256]{1,0:T(8,128)(2,1)} %copy-done.25, bf16[5,832,512]{2,1,0:T(8,128)(2,1)} %get-tuple-element.69.refs_2_, ...), custom_call_target="tpu_custom_call" | custom-call | flops 6543114240 | bytes 8388608 | tf_op jit(solution)/shard_map/backward_5/pallas_call | solution.py:339
  298.7 2.1 collective-permute-start.7
  302.3 10.3 %weights_5.1 = f32[512,1296]{1,0:T(8,128)} custom-call(f32[512,1296]{1,0:T(8,128)} %weights_10.1.refs_0_, bf16[2560,512]{1,0:T(8,128)(2,1)} %bitcast.165, bf16[5,3,576,128]{3,2,1,0:T(8,128)(2,1)} %get-tuple-element.86.refs_2_, bf16[5,512,144]{2,1,0:T(8,128)(2,1)} %get-tuple-element.87.refs_3_, ...), custom_call_target="tpu_custom_call" | custom-call | flops 3397386240 | bytes 16777216 | tf_op jit(solution)/shard_map/weights_5/pallas_call | solution.py:395
  313.9 17.2 %backward_0.1 = (bf16[5,512,512]{2,1,0:T(8,128)(2,1)}, f32[56,128]{1,0:T(8,128)}, f32[16,256]{1,0:T(8,128)}, f32[512,256]{1,0:T(8,128)}, bf16[320,256]{1,0:T(8,128)(2,1)}) custom-call(f32[512,256]{1,0:T(8,128)} %get-tuple-element.72.refs_0_, bf16[320,256]{1,0:T(8,128)(2,1)} %copy-done.23, bf16[5,832,512]{2,1,0:T(8,128)(2,1)} %get-tuple-element.74.refs_2_, ...), custom_call_target="tpu_custom_call" | custom-call | flops 6543114240 | bytes 8388608 | tf_op jit(solution)/shard_map/backward_0/pallas_call | solution.py:339
  332.8 9.6 %weights_0.1 = f32[512,1296]{1,0:T(8,128)} custom-call(bf16[2560,512]{1,0:T(8,128)(2,1)} %bitcast.190, bf16[5,3,576,128]{3,2,1,0:T(8,128)(2,1)} %get-tuple-element.77.refs_1_, bf16[5,512,144]{2,1,0:T(8,128)(2,1)} %get-tuple-element.78.refs_2_, bf16[1632,128]{1,0:T(8,128)(2,1)} %broadcast_in_dim.104.refs_6_.refs_8_.refs_3_.refs_4_, ...), custom_call_target="tpu_custom_call" | custom-call | flops 3397386240 | bytes 16777216 | tf_op jit(solution)/shard_map/weights_0/pallas_call | solution.py:395
  342.3 2.3 pad_maximum_fusion
  344.7 2.5 copy-done
  348.2 1.6 collective-permute-start.11
  352.4 3.2 fusion.1
  355.7 1.6 collective-permute-start.9
  357.3 15.4 %collective-permute-done.9 = bf16[1,8,16,2,1296]{4,2,3,1,0:T(8,128)(2,1)S(1)} collective-permute-done((bf16[1,8,16,2,1296]{4,2,3,1,0:T(8,128)(2,1)S(1)}, bf16[1,8,16,2,1296]{4,2,3,1,0:T(8,128)(2,1)S(1)}, u32[]{:S(2)}, u32[]{:S(2)}) %collective-permute-start.9) | collective-permute-done | bytes 663584 | tf_op jit(solution)/shard_map/ppermute | solution.py:447
  377.6 1.5 reshape.405
  379.1 3.9 all-to-all-start.1
  386.2 14.1 %all-to-all-done.1 = bf16[8,2,23026]{2,1,0:T(2,128)(2,1)S(1)} async-done(((bf16[8,2,23026]{2,1,0:T(2,128)(2,1)}), bf16[8,2,23026]{2,1,0:T(2,128)(2,1)S(1)}, u32[]{:S(2)}, u32[]{:S(2)}) %all-to-all-start.1) | async-done | bytes 736864 | tf_op jit(solution)/shard_map/all_to_all | solution.py:609
  401.6 1.9 convert_reduce_fusion
  405.9 1.6 collective-permute-start.12
  408.1 3.3 collective-permute-done.12
  418.4 1.8 pad_maximum_fusion.2
  421.3 2.3 fusion.33
  (197 shorter events, 65.1 us)
Async XLA Ops:
  4.1 8.3 %copy-start.30 = (s32[8]{0:T(128)S(1)}, s32[8]{0:T(128)}, u32[]{:S(2)}) copy-start(s32[8]{0:T(128)} %constant.97.clone) | copy-start | bytes 100
  4.1 9.5 %copy-start.12 = (s32[4096]{0:T(1024)S(1)}, s32[4096]{0:T(1024)}, u32[]{:S(2)}) copy-start(s32[4096]{0:T(1024)} %param.18) | copy-start | bytes 49156
  5.1 76.8 %all-to-all-start = ((bf16[8,2,16,1296]{3,2,1,0:T(8,128)(2,1)}), bf16[8,2,16,1296]{3,2,1,0:T(8,128)(2,1)S(1)}, u32[]{:S(2)}, u32[]{:S(2)}) async-start(bf16[8,2,16,1296]{3,2,1,0:T(8,128)(2,1)} %broadcast_in_dim.100), calls=%async_computation | async-start | bytes 1441792 | tf_op jit(solution)/shard_map/all_to_all | solution.py:497
  46.0 1.5 copy-start.11
  81.8 11.3 %collective-permute-start = (bf16[1,8,2,16,1296]{4,3,2,1,0:T(8,128)(2,1)S(1)}, bf16[1,8,2,16,1296]{4,3,2,1,0:T(8,128)(2,1)S(1)}, u32[]{:S(2)}, u32[]{:S(2)}) collective-permute-start(bf16[1,8,2,16,1296]{4,3,2,1,0:T(8,128)(2,1)S(1)} %bitcast.161), channel_id=1, source_target_pairs={{0,16},{8,24},{16,0},{24,8},{1,17},{9,25},{17,1},{25,9},{2,18},{10... | collective-permute-start | bytes 1990664 | tf_op jit(solution)/shard_map/ppermute | solution.py:422
  93.3 1.5 copy-start.8
  93.3 2.1 copy-start.19
  93.3 4.1 copy-start.5
  94.7 18.2 %collective-permute-start.1 = (bf16[2,8,2,16,1296]{4,3,2,1,0:T(8,128)(2,1)}, bf16[2,8,2,16,1296]{4,3,2,1,0:T(8,128)(2,1)}, u32[]{:S(2)}, u32[]{:S(2)}) collective-permute-start(bf16[2,8,2,16,1296]{4,3,2,1,0:T(8,128)(2,1)} %maximum_bitcast_fusion), channel_id=1, source_target_pairs={{0,8},{8,0},{16,24},{24,16},{1,9},{9,1},{17,25},{25,17},{2,10},{10... | collective-permute-start | bytes 3981320 | tf_op jit(solution)/shard_map/ppermute | solution.py:422
  121.9 19.1 %copy-start.4 = (f32[15,4096]{1,0:T(8,128)S(1)}, f32[15,4096]{1,0:T(8,128)}, u32[]{:S(2)}) copy-start(f32[15,4096]{1,0:T(8,128)} %reshape.382) | copy-start | bytes 737284
  139.2 6.9 %collective-permute-start.2 = (bf16[320,256]{1,0:T(8,128)(2,1)S(1)}, bf16[320,256]{1,0:T(8,128)(2,1)S(1)}, u32[]{:S(2)}, u32[]{:S(2)}) collective-permute-start(bf16[320,256]{1,0:T(8,128)(2,1)S(1)} %slice.263), channel_id=1, source_target_pairs={{2,0},{4,2},{6,4},{7,6},{5,7},{3,5},{1,3},{0,1},{10,8},{12,10},{14... | collective-permute-start | bytes 491528 | tf_op jit(solution)/shard_map/ppermute | solution.py:560
  146.1 0.7 copy-start.27
  164.4 5.8 %collective-permute-start.3 = (bf16[320,256]{1,0:T(8,128)(2,1)S(1)}, bf16[320,256]{1,0:T(8,128)(2,1)S(1)}, u32[]{:S(2)}, u32[]{:S(2)}) collective-permute-start(bf16[320,256]{1,0:T(8,128)(2,1)S(1)} %slice.268), channel_id=1, source_target_pairs={{2,0},{4,2},{6,4},{7,6},{5,7},{3,5},{1,3},{0,1},{10,8},{12,10},{14... | collective-permute-start | bytes 491528 | tf_op jit(solution)/shard_map/ppermute | solution.py:560
  170.2 0.7 copy-start.28
  188.5 8.2 %collective-permute-start.4 = (bf16[320,256]{1,0:T(8,128)(2,1)S(1)}, bf16[320,256]{1,0:T(8,128)(2,1)S(1)}, u32[]{:S(2)}, u32[]{:S(2)}) collective-permute-start(bf16[320,256]{1,0:T(8,128)(2,1)S(1)} %slice.270), channel_id=1, source_target_pairs={{2,0},{4,2},{6,4},{7,6},{5,7},{3,5},{1,3},{0,1},{10,8},{12,10},{14... | collective-permute-start | bytes 491528 | tf_op jit(solution)/shard_map/ppermute | solution.py:560
  196.8 0.7 copy-start.24
  234.6 10.4 %collective-permute-start.5 = (bf16[320,256]{1,0:T(8,128)(2,1)}, bf16[320,256]{1,0:T(8,128)(2,1)S(1)}, u32[]{:S(2)}, u32[]{:S(2)}) collective-permute-start(bf16[320,256]{1,0:T(8,128)(2,1)} %get-tuple-element.63), channel_id=1, source_target_pairs={{0,2},{2,4},{4,6},{6,7},{7,5},{5,3},{3,1},{1,0},{8,10},{10,12},{12... | collective-permute-start | bytes 491528 | tf_op jit(solution)/shard_map/ppermute | solution.py:580
  245.0 0.7 copy-start.26
  266.3 11.1 %collective-permute-start.6 = (bf16[320,256]{1,0:T(8,128)(2,1)}, bf16[320,256]{1,0:T(8,128)(2,1)S(1)}, u32[]{:S(2)}, u32[]{:S(2)}) collective-permute-start(bf16[320,256]{1,0:T(8,128)(2,1)} %get-tuple-element.68), channel_id=1, source_target_pairs={{0,2},{2,4},{4,6},{6,7},{7,5},{5,3},{3,1},{1,0},{8,10},{10,12},{12... | collective-permute-start | bytes 491528 | tf_op jit(solution)/shard_map/ppermute | solution.py:580
  277.4 0.7 copy-start.25
  278.1 22.7 %copy-start.13 = (f32[16,256]{1,0:T(8,128)S(1)}, f32[16,256]{1,0:T(8,128)}, u32[]{:S(2)}) copy-start(f32[16,256]{1,0:T(8,128)} %get-tuple-element.92) | copy-start | bytes 49156
  278.1 22.7 %copy-start.14 = (f32[16,256]{1,0:T(8,128)S(1)}, f32[16,256]{1,0:T(8,128)}, u32[]{:S(2)}) copy-start(f32[16,256]{1,0:T(8,128)} %get-tuple-element.93) | copy-start | bytes 49156
  278.1 23.5 %copy-start.9 = (f32[56,128]{1,0:T(8,128)S(1)}, f32[56,128]{1,0:T(8,128)}, u32[]{:S(2)}) copy-start(f32[56,128]{1,0:T(8,128)} %get-tuple-element.89) | copy-start | bytes 86020
  278.1 23.5 %copy-start.10 = (f32[56,128]{1,0:T(8,128)S(1)}, f32[56,128]{1,0:T(8,128)}, u32[]{:S(2)}) copy-start(f32[56,128]{1,0:T(8,128)} %get-tuple-element.90) | copy-start | bytes 86020
  298.7 14.5 %collective-permute-start.7 = (bf16[320,256]{1,0:T(8,128)(2,1)}, bf16[320,256]{1,0:T(8,128)(2,1)S(1)}, u32[]{:S(2)}, u32[]{:S(2)}) collective-permute-start(bf16[320,256]{1,0:T(8,128)(2,1)} %get-tuple-element.73), channel_id=1, source_target_pairs={{0,2},{2,4},{4,6},{6,7},{7,5},{5,3},{3,1},{1,0},{8,10},{10,12},{12... | collective-permute-start | bytes 491528 | tf_op jit(solution)/shard_map/ppermute | solution.py:580
  313.3 0.7 copy-start.23
  332.7 15.3 %collective-permute-start.10 = (bf16[2,3858]{1,0:T(2,128)(2,1)S(1)}, bf16[2,3858]{1,0:T(2,128)(2,1)S(1)}, u32[]{:S(2)}, u32[]{:S(2)}) collective-permute-start(bf16[2,3858]{1,0:T(2,128)(2,1)S(1)} %pad_maximum_fusion.4), channel_id=1, source_target_pairs={{0,8},{8,0},{16,24},{24,16},{1,9},{9,1},{17,25},{25,17},{2,10},{10... | collective-permute-start | bytes 46304 | tf_op jit(solution)/shard_map/ppermute | solution.py:450
  332.8 9.6 %copy-start.1 = (f32[512,1296]{1,0:T(8,128)S(1)}, f32[512,1296]{1,0:T(8,128)}, u32[]{:S(2)}) copy-start(f32[512,1296]{1,0:T(8,128)} %weights_5.1) | copy-start | bytes 7962628
  344.7 2.5 copy-start
  347.5 4.9 %collective-permute-start.8 = (bf16[2,8,16,2,1296]{4,2,3,1,0:T(8,128)(2,1)S(1)}, bf16[2,8,16,2,1296]{4,2,3,1,0:T(8,128)(2,1)S(1)}, u32[]{:S(2)}, u32[]{:S(2)}) collective-permute-start(bf16[2,8,16,2,1296]{4,2,3,1,0:T(8,128)(2,1)S(1)} %fusion.2), channel_id=1, source_target_pairs={{0,8},{8,0},{16,24},{24,16},{1,9},{9,1},{17,25},{25,17},{2,10},{10... | collective-permute-start | bytes 3981320 | tf_op jit(solution)/shard_map/ppermute | solution.py:447
  348.2 3.8 collective-permute-start.11
  355.7 17.0 %collective-permute-start.9 = (bf16[1,8,16,2,1296]{4,2,3,1,0:T(8,128)(2,1)S(1)}, bf16[1,8,16,2,1296]{4,2,3,1,0:T(8,128)(2,1)S(1)}, u32[]{:S(2)}, u32[]{:S(2)}) collective-permute-start(bf16[1,8,16,2,1296]{4,2,3,1,0:T(8,128)(2,1)S(1)} %select_convert_fusion.1), channel_id=1, source_target_pairs={{0,16},{8,24},{16,0},{24,8},{1,17},{9,25},{17,1},{25,9},{2,18},{10... | collective-permute-start | bytes 1990664 | tf_op jit(solution)/shard_map/ppermute | solution.py:447
  377.5 5.5 %copy-start.29 = (s32[4]{0:T(128)S(1)}, s32[4]{0:T(128)}, u32[]{:S(2)}) copy-start(s32[4]{0:T(128)} %param.20) | copy-start | bytes 52
  379.1 21.2 %all-to-all-start.1 = ((bf16[8,2,23026]{2,1,0:T(2,128)(2,1)}), bf16[8,2,23026]{2,1,0:T(2,128)(2,1)S(1)}, u32[]{:S(2)}, u32[]{:S(2)}) async-start(bf16[8,2,23026]{2,1,0:T(2,128)(2,1)} %reshape.405), calls=%async_computation.1 | async-start | bytes 1474560 | tf_op jit(solution)/shard_map/all_to_all | solution.py:609
  401.6 3.4 copy-start.16
  401.6 5.9 %copy-start.18 = (f32[2,7,16]{2,0,1:T(2,128)S(1)}, f32[2,7,16]{2,0,1:T(2,128)}, u32[]{:S(2)}) copy-start(f32[2,7,16]{2,0,1:T(2,128)} %param.26) | copy-start | bytes 2692
  401.6 5.9 %copy-start.17 = (f32[2,7,16]{2,0,1:T(2,128)S(1)}, f32[2,7,16]{2,0,1:T(2,128)}, u32[]{:S(2)}) copy-start(f32[2,7,16]{2,0,1:T(2,128)} %param.30) | copy-start | bytes 2692
  401.6 5.9 %copy-start.21 = (f32[16]{0:T(128)S(1)}, f32[16]{0:T(128)}, u32[]{:S(2)}) copy-start(f32[16]{0:T(128)} %param.28) | copy-start | bytes 196
  403.5 8.3 %copy-start.22 = (f32[16]{0:T(128)S(1)}, f32[16]{0:T(128)}, u32[]{:S(2)}) copy-start(f32[16]{0:T(128)} %param.32) | copy-start | bytes 196
  403.5 11.9 %copy-start.15 = (f32[16,128]{1,0:T(8,128)S(1)}, f32[16,128]{1,0:T(8,128)}, u32[]{:S(2)}) copy-start(f32[16,128]{1,0:T(8,128)} %param.31) | copy-start | bytes 24580
  405.6 10.6 %copy-start.7 = (f32[16,128]{1,0:T(8,128)}, f32[16,128]{1,0:T(8,128)S(1)}, u32[]{:S(2)}) copy-start(f32[16,128]{1,0:T(8,128)S(1)} %get-tuple-element.169) | copy-start | bytes 24580
  405.9 5.6 %collective-permute-start.12 = (f32[1,16,2,1296]{3,2,1,0:T(2,128)S(1)}, f32[1,16,2,1296]{3,2,1,0:T(2,128)S(1)}, u32[]{:S(2)}, u32[]{:S(2)}) collective-permute-start(f32[1,16,2,1296]{3,2,1,0:T(2,128)S(1)} %reshape.394), channel_id=1, source_target_pairs={{0,16},{8,24},{16,0},{24,8},{1,17},{9,25},{17,1},{25,9},{2,18},{10... | collective-permute-start | bytes 497672 | tf_op jit(solution)/shard_map/ppermute | solution.py:422
  408.1 8.2 %copy-start.20 = (f32[16]{0:T(128)}, f32[16]{0:T(128)S(1)}, u32[]{:S(2)}) copy-start(f32[16]{0:T(128)S(1)} %get-tuple-element.166) | copy-start | bytes 196
  411.7 4.3 collective-permute-start.13
  420.2 1.1 copy-start.3
  421.3 2.3 copy-start.6
  423.6 1.1 copy-start.2
